TPU v7x, 32 devices: a whole 2x2x4 slice. The times are simulated.
32 devices in a mesh: space: 16 (over z, y, core), slab: 2 (over x).
Axes of the slice: x: 2, y: 2, z: 4, core: 2. Of those that a mesh axis runs over, the one named last changes fastest.
Arguments:
- wavefunctions: bfloat16 [64, 83232], P(None, ('space', 'slab')), may hold values from -6 to 6
- kinetic: bfloat16 [729, 729], replicated, may hold values from -1 to 2, as said below
- cell_scale: float32 [128], P(('space', 'slab')), may hold values from 0.5 to 2
- potential: float32 [128, 729], P(('space', 'slab')), may hold values from -1 to 1
- cell_nodes: int32 [128, 729], P(('space', 'slab')), may hold values from 0 to 2600, as said below
- face_space: int32 [64, 289], P(('space', 'slab')), may hold values from 0 to 2600, as said below
- face_slab: int32 [64, 153], P(('space', 'slab')), may hold values from 0 to 2600, as said below
- projectors: bfloat16 [128, 18, 729], P(('space', 'slab')), may hold values from -0.21875 to 0.21875
- cell_atom: int32 [128], P(('space', 'slab')), may hold values from 0 to 7
- coupling: float32 [128, 18, 18], P(('space', 'slab')), may hold values from -8 to 8
Outputs:
- filtered: float32 [64, 83232], P(None, ('space', 'slab'))
Inputs may be any that keep to these rules, and one draw needn't show every extreme that they name: `cell_nodes`: each block's 4 cells tile a block of 1 x 2 x 2 cells of degree 8; within a block the cell nodes name the nodes of that block's node grid, numbered in an order of the block's own. `face_space`: row 2b lists the nodes of block b's lower face across the long direction and row 2b + 1 those of its upper face, both in one fixed order of the face's positions, so that a block's upper face and the next block's lower face list the same nodes at equal positions; each row names distinct nodes. `face_slab`: likewise for the faces across the cross-section between blocks l and l + 1 of a row. `kinetic`: A symmetric matrix.
All inputs are finite; a program needn't handle non-finite values.
Results may differ from a plain program's by a relative error of at most 0.0039.
Values may be sent and summed in bfloat16 or wider, within the bound.
A program may use at most 64 MiB of HBM per device.

v0:
```python
import functools

import jax
import jax.numpy as jnp
from jax import lax
from jax.experimental import pallas as pl
from jax.experimental.pallas import tpu as pltpu
from jax.sharding import PartitionSpec as P

filter_centre = 8.0
filter_half = 8.0
BLK = 256
MESH = pl.DeviceIdType.MESH
NT = (((1,), (1,)), ((), ()))
f32 = jnp.float32
bf16 = jnp.bfloat16


def up(value, unit):
    return -(-value // unit) * unit


def kernel(
    dims,
    y_ref,
    kin_ref,
    scale_ref,
    pot_ref,
    cn_ref,
    fs_ref,
    fl_ref,
    pr_ref,
    atom_ref,
    coupling_ref,
    out_ref,
    hot,
    hotf,
    hote,
    dup,
    pack,
    idx,
    kin,
    pp,
    pot,
    cross,
    fcol,
    packs,
    coup,
    yb,
    vals,
    tot,
    asm,
    uhl,
    first_total,
    asm2,
    outg,
    in_space,
    in_slab,
    inc,
    marg,
    pack_send,
    pack_recv,
    marg_send,
    marg_recv,
    face_send,
    face_recv,
):
    n_space, n_slab = dims["n_space"], dims["n_slab"]
    width, nodes, cells, order = dims["width"], dims["nodes"], dims["cells"], dims["order"]
    atoms, nproj, pstride = dims["atoms"], dims["nproj"], dims["pstride"]
    fs, fl = dims["fs"], dims["fl"]
    op, npad = up(order, BLK), up(nodes, BLK)
    fsp, flp = up(fs, 128), up(fl, 128)
    jp = cells * op
    fp = up(2 * fsp + 2 * flp, BLK)
    lp = cells * pstride
    o_sl = 2 * fsp

    s = lax.axis_index("space")
    l = lax.axis_index("slab")
    above, below = lax.rem(s + 1, n_space), lax.rem(s + n_space - 1, n_space)
    right, left = lax.rem(l + 1, n_slab), lax.rem(l + n_slab - 1, n_slab)

    lane_cell = lax.broadcasted_iota(jnp.int32, (8, lp), 1) // pstride
    atom_row = jnp.zeros((8, lp), f32)
    for c in range(cells):
        atom_row = jnp.where(lane_cell == c, atom_ref[c].astype(f32), atom_row)
    pack[...] = jnp.zeros(pack.shape, f32)
    for i in range(atoms):
        part = slice(i * pstride, (i + 1) * pstride)
        pack[i * pstride : i * pstride + nproj, 0:nproj] = coupling_ref[:, i, :]
        once = pack[part, :]
        many = once
        for c in range(1, cells):
            many = many + pltpu.roll(once, c * pstride, 1)
        pack[part, :] = many
    pack[atoms * pstride :, :] = atom_row

    barrier = pltpu.get_barrier_semaphore()
    for d in range(1, n_slab):
        pl.semaphore_signal(
            barrier, inc=1, device_id={"slab": lax.rem(l + d, n_slab)}, device_id_type=MESH
        )
    for t in (above, below):
        pl.semaphore_signal(barrier, inc=1, device_id={"space": t}, device_id_type=MESH)
    idx[...] = jnp.full(idx.shape, -1, jnp.int32)
    for c in range(cells):
        idx[0:1, c * op : c * op + order] = cn_ref[c : c + 1, :]
    for k in range(2):
        idx[0:1, jp + k * fsp : jp + k * fsp + fs] = fs_ref[k : k + 1, :]
        off = jp + o_sl + k * flp
        idx[0:1, off : off + fl] = fl_ref[k : k + 1, :]

    kin[...] = jnp.zeros(kin.shape, bf16)
    kin[0:order, 0:order] = kin_ref[...]
    pp[...] = jnp.zeros(pp.shape, bf16)
    pot[...] = jnp.zeros(pot.shape, f32)
    pot[0:cells, 0:order] = pot_ref[...]
    yb[...] = jnp.zeros(yb.shape, bf16)
    yb[:, 0:nodes] = y_ref[...]
    for c in range(cells):
        pp[c * pstride : c * pstride + nproj, c * op : c * op + order] = pr_ref[:, c, :]

    rows = lax.broadcasted_iota(jnp.int32, (BLK, BLK), 0).astype(f32).astype(bf16)

    def one_hot(index_row, b):
        shifted = (index_row - b * BLK).astype(f32).astype(bf16)
        hit = rows == jnp.broadcast_to(shifted, (BLK, BLK))
        return jnp.where(hit, jnp.ones((), bf16), jnp.zeros((), bf16))

    slab_row = idx[0:1, jp + o_sl : jp + o_sl + 2 * flp].astype(f32)
    slab_row = jnp.where(slab_row < 0, -2.0, slab_row)
    for k in range(fp // 128):
        row = idx[0:1, jp + k * 128 : jp + (k + 1) * 128].astype(f32)
        col = jnp.broadcast_to(row, (128, 128)).T
        col = jnp.where(col < 0, -3.0, col)
        fcol[k * 128 : (k + 1) * 128, :] = col
        if k < 2 * fsp // 128:
            cross[k * 128 : (k + 1) * 128, :] = jnp.where(col[:, 0:1] == slab_row, 1.0, 0.0).astype(bf16)

    per_cell = op // BLK

    def build_gather(j):
        at = pl.ds(pl.multiple_of(j * BLK, BLK), BLK)
        index_row = idx[0:1, at]
        got = jnp.zeros((width, BLK), f32)
        for b in range(npad // BLK):
            part = slice(b * BLK, (b + 1) * BLK)
            block = one_hot(index_row, b)
            hot[part, at] = block
            got += jnp.dot(yb[:, part], block, preferred_element_type=f32)
        row = pl.ds(pl.multiple_of(j // per_cell * width, width), width)
        to = pl.ds(pl.multiple_of(j % per_cell * BLK, BLK), BLK)
        vals[row, to] = got.astype(bf16)
        for h in range(BLK // 128):
            lane = pl.ds(pl.multiple_of(j * BLK + h * 128, 128), 128)
            cell_row = jnp.broadcast_to(idx[0:1, lane].astype(f32), (128, 128))
            for k in range(fp // 128):
                part = slice(k * 128, (k + 1) * 128)
                hote[part, lane] = jnp.where(fcol[part, :] == cell_row, 1.0, 0.0).astype(bf16)

    n_pairs = cells * (cells - 1) // 2
    hop = op // 2

    def build_dup(u):
        q, hf = u // 2, u % 2
        one = q % cells
        two = (one + 1 + q // cells) % cells
        for k in range(hop // 128):
            lane = pl.ds(pl.multiple_of(one * op + hf * hop + k * 128, 128), 128)
            col = jnp.broadcast_to(idx[0:1, lane].astype(f32), (128, 128)).T
            col = jnp.where(col < 0, -2.0, col)
            to = pl.ds(pl.multiple_of(q * op + hf * hop + k * 128, 128), 128)
            for h in range(op // 128):
                lane = pl.ds(pl.multiple_of(two * op + h * 128, 128), 128)
                row = jnp.broadcast_to(idx[0:1, lane].astype(f32), (128, 128))
                dup[to, h * 128 : (h + 1) * 128] = jnp.where(col == row, 1.0, 0.0).astype(bf16)

    together = 2 * n_pairs == cells * per_cell

    def build_all(j):
        build_gather(j)
        if together:
            build_dup(j)

    if not together:
        pl.loop(0, 2 * n_pairs)(build_dup)
    half = cells * per_cell // 2
    pl.loop(0, half)(build_all)
    pl.semaphore_wait(barrier, n_slab + 1)
    pack_copies = []
    for d in range(1, n_slab):
        copy = pltpu.make_async_remote_copy(
            src_ref=pack,
            dst_ref=packs.at[d - 1],
            send_sem=pack_send.at[d - 1],
            recv_sem=pack_recv.at[d - 1],
            device_id={"slab": lax.rem(l + d, n_slab)},
            device_id_type=MESH,
        )
        copy.start()
        pack_copies.append(copy)

    pl.loop(half, cells * per_cell)(build_all)

    for copy in pack_copies:
        copy.wait()
    own_row = pack[atoms * pstride : atoms * pstride + 1, :]
    own_col = jnp.broadcast_to(own_row, (lp, lp)).T
    chosen = jnp.zeros((lp, lp), f32)
    for d in range(n_slab):
        source = lax.rem(l + n_slab - d, n_slab)
        for i in range(atoms):
            part = slice(i * pstride, (i + 1) * pstride)
            block = pack[part, :] if d == 0 else packs[d - 1, part, :]
            tiled = jnp.concatenate([block] * cells, axis=0)
            chosen += jnp.where(own_col == (source * atoms + i).astype(f32), tiled, 0.0)
    for d in range(n_slab):
        last = slice(atoms * pstride, atoms * pstride + 1)
        row = pack[last, :] if d == 0 else packs[d - 1, last, :]
        coup[d] = jnp.where(own_col == row, chosen, 0.0)

    lanes = lax.broadcasted_iota(jnp.int32, (1, fp), 1)
    has_below, has_above = s > 0, s < n_space - 1
    has_left, has_right = l > 0, l < n_slab - 1
    keep = (
        ((lanes < fsp) & has_below)
        | ((lanes >= fsp) & (lanes < o_sl) & has_above)
        | ((lanes >= o_sl) & (lanes < o_sl + flp) & has_left)
        | ((lanes >= o_sl + flp) & (lanes < o_sl + 2 * flp) & has_right)
    ).astype(f32)

    inc[...] = jnp.zeros(inc.shape, bf16)

    def face_copy(step, which, src, landing, device):
        count = landing.shape[-1]
        return pltpu.make_async_remote_copy(
            src_ref=outg.at[step, :, src : src + count],
            dst_ref=landing.at[step, which % 2],
            send_sem=face_send.at[step, which],
            recv_sem=face_recv.at[step, which],
            device_id=device,
            device_id_type=MESH,
        )

    for step in range(2):
        margin = jnp.zeros((width, lp), f32)
        for c in range(cells):
            margin += lax.dot_general(
                vals[c * width : (c + 1) * width, :],
                pp[:, c * op : (c + 1) * op],
                NT,
                preferred_element_type=f32,
            )
        marg[step, 0] = margin
        marg_copies = []
        for d in range(1, n_slab):
            copy = pltpu.make_async_remote_copy(
                src_ref=marg.at[step, 0],
                dst_ref=marg.at[step, d],
                send_sem=marg_send.at[step, d - 1],
                recv_sem=marg_recv.at[step, d - 1],
                device_id={"slab": lax.rem(l + d, n_slab)},
                device_id_type=MESH,
            )
            copy.start()
            marg_copies.append(copy)

        asm_kin = jnp.dot(vals[...], kin[...], preferred_element_type=f32)
        for c in range(cells):
            v = vals[c * width : (c + 1) * width, :].astype(f32)
            asm[:, c * op : (c + 1) * op] = (
                scale_ref[c] * asm_kin[c * width : (c + 1) * width] + pot[c : c + 1, :] * v
            )
        coupled = lax.dot_general(
            margin, coup[0], NT, precision=lax.Precision.HIGHEST, preferred_element_type=f32
        )
        for d in range(1, n_slab):
            marg_copies[d - 1].wait()
            coupled += lax.dot_general(
                marg[step, d], coup[d], NT, precision=lax.Precision.HIGHEST, preferred_element_type=f32
            )
        coupled = coupled.astype(bf16)
        for c in range(cells):
            cols = slice(c * op, (c + 1) * op)
            total = asm[:, cols] + jnp.dot(coupled, pp[:, cols], preferred_element_type=f32)
            high = total.astype(bf16)
            tot[0:width, cols] = high
            tot[width:, cols] = (total - high.astype(f32)).astype(bf16)
            if step == 0:
                first_total[:, cols] = total
            else:
                step_change = 2.0 / filter_half * total - (
                    2.0 * filter_centre / filter_half / filter_half * first_total[:, cols]
                )
                high = step_change.astype(bf16)
                uhl[0:width, cols] = high
                uhl[width:, cols] = (step_change - high.astype(f32)).astype(bf16)

        @pl.loop(0, fp // BLK)
        def _(b):
            to = pl.ds(pl.multiple_of(b * BLK, BLK), BLK)
            both = lax.dot_general(tot[:, 0:jp], hote[to, :], NT, preferred_element_type=f32)
            outg[step, :, to] = (both[0:width] + both[width:]).astype(bf16)

        space_copies = [
            face_copy(step, 0, fsp, in_space, {"space": above}),
            face_copy(step, 1, 0, in_space, {"space": below}),
        ]
        for copy in space_copies:
            copy.start()

        def scatter(b):
            at = pl.ds(pl.multiple_of(b * BLK, BLK), BLK)
            for j in range(fp // BLK):
                hotf[at, j * BLK : (j + 1) * BLK] = one_hot(
                    idx[0:1, jp + j * BLK : jp + (j + 1) * BLK], b
                )
            both = lax.dot_general(uhl[...], hot[at, :], NT, preferred_element_type=f32)
            start = yb[:, at].astype(f32)
            kept = 2.0 * filter_centre * filter_centre / filter_half / filter_half - 1.0
            asm2[:, at] = both[0:width] + both[width:] + kept * start

        def share(c):
            @pl.loop(0, per_cell)
            def _(n):
                to = pl.ds(pl.multiple_of(n * BLK, BLK), BLK)
                both = jnp.zeros((2 * width, BLK), f32)
                for q in range(n_pairs):
                    one = q % cells
                    two = (one + 1 + q // cells) % cells
                    if two == c:
                        both += jnp.dot(
                            tot[:, one * op : (one + 1) * op],
                            dup[q * op : (q + 1) * op, to],
                            preferred_element_type=f32,
                        )
                    elif one == c:
                        rows = pl.ds(pl.multiple_of(q * op + n * BLK, BLK), BLK)
                        both += lax.dot_general(
                            tot[:, two * op : (two + 1) * op],
                            dup[rows, :],
                            NT,
                            preferred_element_type=f32,
                        )
                at = pl.ds(pl.multiple_of(c * op + n * BLK, BLK), BLK)
                value = vals[c * width : (c + 1) * width, to].astype(f32)
                summed = first_total[:, at] + both[0:width] + both[width:]
                asm[:, at] = (summed - filter_centre * value) / filter_half

        blocks = npad // BLK
        if step == 0:
            for c in range(cells // 2):
                share(c)
        else:
            pl.loop(0, blocks // 2)(scatter)

        for k, copy in enumerate(space_copies):
            copy.wait()
            part = slice(k * fsp, (k + 1) * fsp)
            inc[step, :, part] = (in_space[step, k].astype(f32) * keep[:, part]).astype(bf16)
        extra = jnp.dot(inc[step, :, 0:o_sl], cross[...], preferred_element_type=f32)
        part = slice(o_sl, o_sl + 2 * flp)
        outg[step, :, part] = (outg[step, :, part].astype(f32) + extra).astype(bf16)
        slab_copies = [
            face_copy(step, 2, o_sl + flp, in_slab, {"slab": right}),
            face_copy(step, 3, o_sl, in_slab, {"slab": left}),
        ]
        for copy in slab_copies:
            copy.start()

        if step == 0:
            for c in range(cells // 2, cells):
                share(c)
        else:
            pl.loop(blocks // 2, blocks)(scatter)

        for k, copy in enumerate(slab_copies):
            copy.wait()
            part = slice(o_sl + k * flp, o_sl + (k + 1) * flp)
            inc[step, :, part] = (in_slab[step, k].astype(f32) * keep[:, part]).astype(bf16)

        if step == 0:
            @pl.loop(0, cells * per_cell)
            def _(j):
                at = pl.ds(pl.multiple_of(j * BLK, BLK), BLK)
                added = jnp.dot(inc[0], hote[:, at], preferred_element_type=f32)
                row = pl.ds(pl.multiple_of(j // per_cell * width, width), width)
                to = pl.ds(pl.multiple_of(j % per_cell * BLK, BLK), BLK)
                vals[row, to] = (asm[:, at] + added / filter_half).astype(bf16)

    change = (
        2.0 / filter_half * inc[1].astype(f32)
        - 2.0 * filter_centre / filter_half / filter_half * inc[0].astype(f32)
    )
    high = change.astype(bf16)
    tot[0:width, 0:fp] = high
    tot[width:, 0:fp] = (change - high.astype(f32)).astype(bf16)

    def final(at):
        both = lax.dot_general(tot[:, 0:fp], hotf[at, :], NT, preferred_element_type=f32)
        return asm2[:, at] + both[0:width] + both[width:]

    @pl.loop(0, nodes // BLK)
    def _(b):
        at = pl.ds(pl.multiple_of(b * BLK, BLK), BLK)
        out_ref[:, at] = final(at)

    if nodes % BLK:
        low = nodes // BLK * BLK
        out_ref[:, low:nodes] = final(slice(low, low + BLK))[:, 0 : nodes - low]


def shards(
    wavefunctions,
    kinetic,
    cell_scale,
    potential,
    cell_nodes,
    face_space,
    face_slab,
    projectors,
    cell_atom,
    coupling,
):
    width, nodes = wavefunctions.shape
    cells, order = cell_nodes.shape
    atoms, nproj = coupling.shape[0], coupling.shape[1]
    n_space, n_slab = lax.axis_size("space"), lax.axis_size("slab")
    fs, fl = face_space.shape[1], face_slab.shape[1]
    pstride = up(nproj, 16)
    while cells * pstride % 128:
        pstride += 16
    dims = dict(
        n_space=n_space, n_slab=n_slab, width=width, nodes=nodes, cells=cells, order=order,
        atoms=atoms, nproj=nproj, pstride=pstride, fs=fs, fl=fl,
    )
    op, npad = up(order, BLK), up(nodes, BLK)
    fsp, flp = up(fs, 128), up(fl, 128)
    jp = cells * op
    fp = up(2 * fsp + 2 * flp, BLK)
    lp = cells * pstride
    others = max(n_slab - 1, 1)
    vmem = pl.BlockSpec(memory_space=pltpu.VMEM)
    smem = pl.BlockSpec(memory_space=pltpu.SMEM)
    dma = pltpu.SemaphoreType.DMA
    return pl.pallas_call(
        functools.partial(kernel, dims),
        out_shape=jax.ShapeDtypeStruct((width, nodes), f32),
        in_specs=[vmem, vmem, smem] + [vmem] * 5 + [smem, vmem],
        out_specs=vmem,
        scratch_shapes=[
            pltpu.VMEM((npad, jp), bf16),
            pltpu.VMEM((npad, fp), bf16),
            pltpu.VMEM((fp, jp), bf16),
            pltpu.VMEM((cells * (cells - 1) // 2 * op, op), bf16),
            pltpu.VMEM((atoms * pstride + 8, lp), f32),
            pltpu.VMEM((8, jp + fp), jnp.int32),
            pltpu.VMEM((op, op), bf16),
            pltpu.VMEM((lp, jp), bf16),
            pltpu.VMEM((up(cells, 8), op), f32),
            pltpu.VMEM((2 * fsp, 2 * flp), bf16),
            pltpu.VMEM((fp, 128), f32),
            pltpu.VMEM((others, atoms * pstride + 8, lp), f32),
            pltpu.VMEM((n_slab, lp, lp), f32),
            pltpu.VMEM((width, npad), bf16),
            pltpu.VMEM((cells * width, op), bf16),
            pltpu.VMEM((2 * width, max(jp, fp)), bf16),
            pltpu.VMEM((width, jp), f32),
            pltpu.VMEM((2 * width, jp), bf16),
            pltpu.VMEM((width, jp), f32),
            pltpu.VMEM((width, npad), f32),
            pltpu.VMEM((2, width, fp), bf16),
            pltpu.VMEM((2, 2, width, fsp), bf16),
            pltpu.VMEM((2, 2, width, flp), bf16),
            pltpu.VMEM((2, width, fp), bf16),
            pltpu.VMEM((2, n_slab, width, lp), f32),
            dma((others,)),
            dma((others,)),
            dma((2, others)),
            dma((2, others)),
            dma((2, 4)),
            dma((2, 4)),
        ],
        compiler_params=pltpu.CompilerParams(
            collective_id=0, has_side_effects=True, vmem_limit_bytes=60 * 1024 * 1024
        ),
    )(
        wavefunctions, kinetic, cell_scale, potential, cell_nodes, face_space, face_slab,
        projectors.transpose(1, 0, 2), cell_atom, coupling.transpose(1, 0, 2),
    )


def solution(mesh):
    placed = (
        P(None, ("space", "slab")),
        P(),
        P(("space", "slab")),
        P(("space", "slab"), None),
        P(("space", "slab"), None),
        P(("space", "slab"), None),
        P(("space", "slab"), None),
        P(("space", "slab"), None, None),
        P(("space", "slab")),
        P(("space", "slab"), None, None),
    )
    return jax.shard_map(
        shards, mesh=mesh, in_specs=placed, out_specs=P(None, ("space", "slab")), check_vma=False
    )
```

profile of v0, /device:TPU:0, one launch (start us, length us, event | category | flops | bytes accessed | tf_op | source)
XLA Modules:
  0.0 54.6 jit_solution(12772348319676841682)
XLA Ops:
  0.0 52.6 %shard_map.100 = f32[64,2601]{1,0:T(8,128)} custom-call(bf16[64,2601]{1,0:T(8,128)(2,1)} %y_ref.1, bf16[729,729]{1,0:T(8,128)(2,1)} %kin_ref.1, f32[4]{0:T(128)} %scale_ref.1, f32[4,729]{1,0:T(4,128)} %pot_ref.1, s32[4,729]{1,0:T(4,128)} %cn_ref.1, s32[2,289]{1,0:T(2,128)} %fs_ref.1, s32[2,153]{1,0:T(2,128)} %fl_ref.1, bf16[18,4,729]{2,1,0:T(4,128)(2,1)} %bitcast.2, ...), custom_call_target="tpu_custom_call" | custom-call | tf_op jit(solution)/shard_map/pallas_call | solution.py:447
  52.6 2.0 %copy.12 = f32[64,2601]{1,0:T(8,128)} copy(f32[64,2601]{1,0:T(8,128)} %shard_map.100) | data formatting | bytes 1331712
where the time goes:
time: 54.8 us; the launch traced here: 54.6 us
  Pallas kernels  52.6 us (96%)
  local copies, waits for them, and re-layouts  1.99 us (4%)
    pallas_call x1, Pallas kernels, shards(): pl.pallas_call(functools.partial(kernel, dims), out_shape=jax.ShapeDtypeS...  52.6 us
    unnamed x1, local copies, waits for them, and re-layouts  1.99 us

commit v1 on v0

v1 whole, which is shorter than its diff:
```python
import functools

import jax
import jax.numpy as jnp
from jax import lax
from jax.experimental import pallas as pl
from jax.experimental.pallas import tpu as pltpu
from jax.sharding import PartitionSpec as P

filter_centre = 8.0
filter_half = 8.0
BLK = 256
SHIFT = 8
MESH = pl.DeviceIdType.MESH
NT = (((1,), (1,)), ((), ()))
f32 = jnp.float32
bf16 = jnp.bfloat16


def up(value, unit):
    return -(-value // unit) * unit


def kernel(
    dims,
    y_ref,
    kin_ref,
    scale_ref,
    pot_ref,
    cn_ref,
    fs_ref,
    fl_ref,
    pr_ref,
    atom_ref,
    coupling_ref,
    out_ref,
    hot,
    pack,
    idx,
    kin,
    pp,
    pot,
    cross,
    packs,
    coup,
    yb,
    vals,
    kinv,
    tot,
    asm,
    field,
    outg,
    in_space,
    in_slab,
    inc,
    marg,
    pack_send,
    pack_recv,
    marg_send,
    marg_recv,
    face_send,
    face_recv,
):
    n_space, n_slab = dims["n_space"], dims["n_slab"]
    width, nodes, cells, order = dims["width"], dims["nodes"], dims["cells"], dims["order"]
    atoms, nproj, pstride = dims["atoms"], dims["nproj"], dims["pstride"]
    fs, fl = dims["fs"], dims["fl"]
    op, npad = up(order, BLK), up(nodes, BLK)
    fsp, flp = up(fs, 128), up(fl, 128)
    jp = cells * op
    fp = up(2 * fsp + 2 * flp, BLK)
    lp = cells * pstride
    o_sl = 2 * fsp
    blocks = npad // BLK

    s = lax.axis_index("space")
    l = lax.axis_index("slab")
    above, below = lax.rem(s + 1, n_space), lax.rem(s + n_space - 1, n_space)
    right, left = lax.rem(l + 1, n_slab), lax.rem(l + n_slab - 1, n_slab)

    lane_cell = lax.broadcasted_iota(jnp.int32, (8, lp), 1) // pstride
    atom_row = jnp.zeros((8, lp), f32)
    for c in range(cells):
        atom_row = jnp.where(lane_cell == c, atom_ref[c].astype(f32), atom_row)
    pack[...] = jnp.zeros(pack.shape, f32)
    for i in range(atoms):
        part = slice(i * pstride, (i + 1) * pstride)
        pack[i * pstride : i * pstride + nproj, 0:nproj] = coupling_ref[:, i, :]
        once = pack[part, :]
        many = once
        for c in range(1, cells):
            many = many + pltpu.roll(once, c * pstride, 1)
        pack[part, :] = many
    pack[atoms * pstride :, :] = atom_row

    barrier = pltpu.get_barrier_semaphore()
    for d in range(1, n_slab):
        pl.semaphore_signal(
            barrier, inc=1, device_id={"slab": lax.rem(l + d, n_slab)}, device_id_type=MESH
        )
    for t in (above, below):
        pl.semaphore_signal(barrier, inc=1, device_id={"space": t}, device_id_type=MESH)
    idx[...] = jnp.full(idx.shape, -1, jnp.int32)
    for c in range(cells):
        idx[0:1, c * op : c * op + order] = cn_ref[c : c + 1, :]
    for k in range(2):
        idx[0:1, jp + k * fsp : jp + k * fsp + fs] = fs_ref[k : k + 1, :]
        off = jp + o_sl + k * flp
        idx[0:1, off : off + fl] = fl_ref[k : k + 1, :]

    for b in range(blocks):
        count = min(BLK, nodes - b * BLK)
        rows = slice(b * width, (b + 1) * width)
        if count < BLK:
            yb[rows, :] = jnp.zeros((width, BLK), bf16)
        yb[rows, 0:count] = y_ref[:, b * BLK : b * BLK + count]
    kin[...] = jnp.zeros(kin.shape, bf16)
    kin[0:order, 0:order] = kin_ref[...]
    pp[...] = jnp.zeros(pp.shape, bf16)
    pot[...] = jnp.zeros(pot.shape, f32)
    pot[0:cells, 0:order] = pot_ref[...]
    for c in range(cells):
        pp[c * pstride : c * pstride + nproj, c * op : c * op + order] = pr_ref[:, c, :]

    lane_rows = lax.broadcasted_iota(jnp.int32, (BLK, BLK), 0).astype(f32).astype(bf16)

    def tile(start):
        if isinstance(start, int):
            return slice(start, start + BLK)
        return pl.ds(pl.multiple_of(start, BLK), BLK)

    def low_part(at):
        low = (idx[0:1, at] & (BLK - 1)).astype(f32).astype(bf16)
        hit = lane_rows == jnp.broadcast_to(low, (BLK, BLK))
        return jnp.where(hit, jnp.ones((), bf16), jnp.zeros((), bf16))

    def gather(source, at):
        every = jnp.dot(source[...], hot[:, at], preferred_element_type=f32)
        high = jnp.broadcast_to(idx[0:1, at] >> SHIFT, (width, BLK))
        got = jnp.zeros((width, BLK), f32)
        for b in range(blocks):
            got = jnp.where(high == b, every[b * width : (b + 1) * width], got)
        return got.astype(bf16)

    def spread(pieces):
        left_side, right_side = [], []
        for value, at in pieces:
            high = (idx[0:1, at] >> SHIFT).astype(f32).astype(bf16)
            high = jnp.broadcast_to(high, (width, BLK))
            none = jnp.zeros((), bf16)
            left_side.append(
                jnp.concatenate(
                    [jnp.where(high == jnp.full((), b, bf16), value, none) for b in range(blocks)], axis=0
                )
            )
            right_side.append(hot[:, at])
        return lax.dot_general(
            jnp.concatenate(left_side, axis=1),
            jnp.concatenate(right_side, axis=1),
            NT,
            preferred_element_type=f32,
        )

    per_cell = op // BLK
    tiles = cells * per_cell
    group = 2 if tiles % 2 == 0 else 1

    def take_cells(source, build):
        def body(i):
            for u in range(group):
                j = i * group + u
                at = tile(j * BLK)
                if build:
                    hot[:, at] = low_part(at)
                row = pl.ds(pl.multiple_of(j // per_cell * width, width), width)
                vals[row, tile(j % per_cell * BLK)] = gather(source, at)

        return body

    for k in range(fp // BLK):
        at = tile(jp + k * BLK)
        hot[:, at] = low_part(at)
    slab_row = idx[0:1, jp + o_sl : jp + o_sl + 2 * flp].astype(f32)
    slab_row = jnp.where(slab_row < 0, -2.0, slab_row)
    for k in range(2 * fsp // 128):
        row = idx[0:1, jp + k * 128 : jp + (k + 1) * 128].astype(f32)
        col = jnp.broadcast_to(row, (128, 128)).T
        cross[k * 128 : (k + 1) * 128, :] = jnp.where(col[:, 0:1] == slab_row, 1.0, 0.0).astype(bf16)

    pl.semaphore_wait(barrier, n_slab + 1)
    pack_copies = []
    for d in range(1, n_slab):
        copy = pltpu.make_async_remote_copy(
            src_ref=pack,
            dst_ref=packs.at[d - 1],
            send_sem=pack_send.at[d - 1],
            recv_sem=pack_recv.at[d - 1],
            device_id={"slab": lax.rem(l + d, n_slab)},
            device_id_type=MESH,
        )
        copy.start()
        pack_copies.append(copy)

    pl.loop(0, tiles // group)(take_cells(yb, True))

    for copy in pack_copies:
        copy.wait()
    own_row = pack[atoms * pstride : atoms * pstride + 1, :]
    own_col = jnp.broadcast_to(own_row, (lp, lp)).T
    chosen = jnp.zeros((lp, lp), f32)
    for d in range(n_slab):
        source = lax.rem(l + n_slab - d, n_slab)
        for i in range(atoms):
            part = slice(i * pstride, (i + 1) * pstride)
            block = pack[part, :] if d == 0 else packs[d - 1, part, :]
            tiled = jnp.concatenate([block] * cells, axis=0)
            chosen += jnp.where(own_col == (source * atoms + i).astype(f32), tiled, 0.0)
    for d in range(n_slab):
        last = slice(atoms * pstride, atoms * pstride + 1)
        row = pack[last, :] if d == 0 else packs[d - 1, last, :]
        coup[d] = jnp.where(own_col == row, chosen, 0.0)

    lanes = lax.broadcasted_iota(jnp.int32, (1, fp), 1)
    has_below, has_above = s > 0, s < n_space - 1
    has_left, has_right = l > 0, l < n_slab - 1
    keep = (
        ((lanes < fsp) & has_below)
        | ((lanes >= fsp) & (lanes < o_sl) & has_above)
        | ((lanes >= o_sl) & (lanes < o_sl + flp) & has_left)
        | ((lanes >= o_sl + flp) & (lanes < o_sl + 2 * flp) & has_right)
    ).astype(f32)

    inc[...] = jnp.zeros(inc.shape, bf16)

    def face_copy(step, which, src, landing, device):
        count = landing.shape[-1]
        return pltpu.make_async_remote_copy(
            src_ref=outg.at[step, :, src : src + count],
            dst_ref=landing.at[step, which % 2],
            send_sem=face_send.at[step, which],
            recv_sem=face_recv.at[step, which],
            device_id=device,
            device_id_type=MESH,
        )

    for step in range(2):
        if step == 1:
            pl.loop(0, tiles // group)(take_cells(yb, False))
        margin = jnp.zeros((width, lp), f32)
        for c in range(cells):
            margin += lax.dot_general(
                vals[c * width : (c + 1) * width, :],
                pp[:, c * op : (c + 1) * op],
                NT,
                preferred_element_type=f32,
            )
        marg[step, 0] = margin
        marg_copies = []
        for d in range(1, n_slab):
            copy = pltpu.make_async_remote_copy(
                src_ref=marg.at[step, 0],
                dst_ref=marg.at[step, d],
                send_sem=marg_send.at[step, d - 1],
                recv_sem=marg_recv.at[step, d - 1],
                device_id={"slab": lax.rem(l + d, n_slab)},
                device_id_type=MESH,
            )
            copy.start()
            marg_copies.append(copy)

        kinv[...] = jnp.dot(vals[...], kin[...], preferred_element_type=f32)
        coupled = lax.dot_general(
            margin, coup[0], NT, precision=lax.Precision.HIGHEST, preferred_element_type=f32
        )
        for d in range(1, n_slab):
            marg_copies[d - 1].wait()
            coupled += lax.dot_general(
                marg[step, d], coup[d], NT, precision=lax.Precision.HIGHEST, preferred_element_type=f32
            )
        coupled = coupled.astype(bf16)
        for c in range(cells):
            cols = slice(c * op, (c + 1) * op)
            rows = slice(c * width, (c + 1) * width)
            total = jnp.dot(coupled, pp[:, cols], preferred_element_type=f32)
            total += scale_ref[c] * kinv[rows, :] + pot[c : c + 1, :] * vals[rows, :].astype(f32)
            tot[rows, :] = total.astype(bf16)

        asm[...] = jnp.zeros(asm.shape, f32)

        @pl.loop(0, cells)
        def _(c):
            row = pl.ds(pl.multiple_of(c * width, width), width)
            asm[...] += spread(
                [(tot[row, tile(n * BLK)], tile(c * op + n * BLK)) for n in range(per_cell)]
            )

        yb[...] = asm[...].astype(bf16)

        def take_faces(first, last):
            for k in range(first // BLK, last // BLK):
                outg[step, :, tile(k * BLK)] = gather(yb, tile(jp + k * BLK))

        cut = up(o_sl, BLK)
        take_faces(0, cut)
        space_copies = [
            face_copy(step, 0, fsp, in_space, {"space": above}),
            face_copy(step, 1, 0, in_space, {"space": below}),
        ]
        for copy in space_copies:
            copy.start()
        take_faces(cut, fp)

        if step == 0:
            for b in range(blocks):
                rows = slice(b * width, (b + 1) * width)
                count = min(BLK, nodes - b * BLK)
                field[rows, 0:count] = asm[rows, 0:count] - filter_centre * y_ref[
                    :, b * BLK : b * BLK + count
                ].astype(f32)
                if count < BLK:
                    field[rows, count:] = jnp.zeros((width, BLK - count), f32)
        else:
            for b in range(blocks):
                rows = slice(b * width, (b + 1) * width)
                count = min(BLK, nodes - b * BLK)
                start = y_ref[:, b * BLK : b * BLK + count].astype(f32)
                asm[rows, 0:count] = (
                    2.0 / filter_half * asm[rows, 0:count]
                    - 2.0 * filter_centre / filter_half * field[rows, 0:count]
                    - start
                )

        for k, copy in enumerate(space_copies):
            copy.wait()
            part = slice(k * fsp, (k + 1) * fsp)
            inc[step, :, part] = (in_space[step, k].astype(f32) * keep[:, part]).astype(bf16)
        extra = jnp.dot(inc[step, :, 0:o_sl], cross[...], preferred_element_type=f32)
        part = slice(o_sl, o_sl + 2 * flp)
        outg[step, :, part] = (outg[step, :, part].astype(f32) + extra).astype(bf16)
        slab_copies = [
            face_copy(step, 2, o_sl + flp, in_slab, {"slab": right}),
            face_copy(step, 3, o_sl, in_slab, {"slab": left}),
        ]
        for copy in slab_copies:
            copy.start()

        def add_faces(first, last):
            return spread(
                [
                    (inc[step, :, tile(k * BLK)], tile(jp + k * BLK))
                    for k in range(first // BLK, last // BLK)
                ]
            )

        whole = o_sl // BLK * BLK
        gain = 1.0 if step == 0 else 2.0 / filter_half
        into = field if step == 0 else asm
        if whole:
            into[...] += gain * add_faces(0, whole)

        for k, copy in enumerate(slab_copies):
            copy.wait()
            part = slice(o_sl + k * flp, o_sl + (k + 1) * flp)
            inc[step, :, part] = (in_slab[step, k].astype(f32) * keep[:, part]).astype(bf16)
        rest = into[...] + gain * add_faces(whole, fp)
        if step == 0:
            rest = rest / filter_half
            field[...] = rest
            yb[...] = rest.astype(bf16)
        else:
            for b in range(blocks):
                count = min(BLK, nodes - b * BLK)
                out_ref[:, b * BLK : b * BLK + count] = rest[b * width : (b + 1) * width, 0:count]


def shards(
    wavefunctions,
    kinetic,
    cell_scale,
    potential,
    cell_nodes,
    face_space,
    face_slab,
    projectors,
    cell_atom,
    coupling,
):
    width, nodes = wavefunctions.shape
    cells, order = cell_nodes.shape
    atoms, nproj = coupling.shape[0], coupling.shape[1]
    n_space, n_slab = lax.axis_size("space"), lax.axis_size("slab")
    fs, fl = face_space.shape[1], face_slab.shape[1]
    pstride = up(nproj, 16)
    while cells * pstride % 128:
        pstride += 16
    dims = dict(
        n_space=n_space, n_slab=n_slab, width=width, nodes=nodes, cells=cells, order=order,
        atoms=atoms, nproj=nproj, pstride=pstride, fs=fs, fl=fl,
    )
    op, npad = up(order, BLK), up(nodes, BLK)
    fsp, flp = up(fs, 128), up(fl, 128)
    jp = cells * op
    fp = up(2 * fsp + 2 * flp, BLK)
    lp = cells * pstride
    others = max(n_slab - 1, 1)
    vmem = pl.BlockSpec(memory_space=pltpu.VMEM)
    smem = pl.BlockSpec(memory_space=pltpu.SMEM)
    dma = pltpu.SemaphoreType.DMA
    return pl.pallas_call(
        functools.partial(kernel, dims),
        out_shape=jax.ShapeDtypeStruct((width, nodes), f32),
        in_specs=[vmem, vmem, smem] + [vmem] * 5 + [smem, vmem],
        out_specs=vmem,
        scratch_shapes=[
            pltpu.VMEM((BLK, jp + fp), bf16),
            pltpu.VMEM((atoms * pstride + 8, lp), f32),
            pltpu.VMEM((8, jp + fp), jnp.int32),
            pltpu.VMEM((op, op), bf16),
            pltpu.VMEM((lp, jp), bf16),
            pltpu.VMEM((up(cells, 8), op), f32),
            pltpu.VMEM((2 * fsp, 2 * flp), bf16),
            pltpu.VMEM((others, atoms * pstride + 8, lp), f32),
            pltpu.VMEM((n_slab, lp, lp), f32),
            pltpu.VMEM((npad // BLK * width, BLK), bf16),
            pltpu.VMEM((cells * width, op), bf16),
            pltpu.VMEM((cells * width, op), f32),
            pltpu.VMEM((cells * width, op), bf16),
            pltpu.VMEM((npad // BLK * width, BLK), f32),
            pltpu.VMEM((npad // BLK * width, BLK), f32),
            pltpu.VMEM((2, width, fp), bf16),
            pltpu.VMEM((2, 2, width, fsp), bf16),
            pltpu.VMEM((2, 2, width, flp), bf16),
            pltpu.VMEM((2, width, fp), bf16),
            pltpu.VMEM((2, n_slab, width, lp), f32),
            dma((others,)),
            dma((others,)),
            dma((2, others)),
            dma((2, others)),
            dma((2, 4)),
            dma((2, 4)),
        ],
        compiler_params=pltpu.CompilerParams(
            collective_id=0, has_side_effects=True, vmem_limit_bytes=60 * 1024 * 1024
        ),
    )(
        wavefunctions, kinetic, cell_scale, potential, cell_nodes, face_space, face_slab,
        projectors.transpose(1, 0, 2), cell_atom, coupling.transpose(1, 0, 2),
    )


def solution(mesh):
    placed = (
        P(None, ("space", "slab")),
        P(),
        P(("space", "slab")),
        P(("space", "slab"), None),
        P(("space", "slab"), None),
        P(("space", "slab"), None),
        P(("space", "slab"), None),
        P(("space", "slab"), None, None),
        P(("space", "slab")),
        P(("space", "slab"), None, None),
    )
    return jax.shard_map(
        shards, mesh=mesh, in_specs=placed, out_specs=P(None, ("space", "slab")), check_vma=False
    )
```

time: 54.8 us -> 44.5 us (0.81)
  Pallas kernels: 52.6 us -> 42.4 us
    pallas_call x1, Pallas kernels: 52.6 us -> 42.4 us  [shards(): pl.pallas_call(functools.partial(kernel, dims), out_shape=jax.ShapeDtypeS...]
where the time goes in v1:
time: 44.5 us; the launch traced here: 44.4 us
  Pallas kernels  42.4 us (95%)
  local copies, waits for them, and re-layouts  1.99 us (4%)
    pallas_call x1, Pallas kernels, shards(): pl.pallas_call(functools.partial(kernel, dims), out_shape=jax.ShapeDtypeS...  42.4 us
    unnamed x1, local copies, waits for them, and re-layouts  1.99 us

profile of v1, /device:TPU:0, one launch (start us, length us, event | category | flops | bytes accessed | tf_op | source)
XLA Modules:
  0.0 44.4 jit_solution(11856085036215336492)
XLA Ops:
  0.0 42.4 %shard_map.100 = f32[64,2601]{1,0:T(8,128)} custom-call(bf16[64,2601]{1,0:T(8,128)(2,1)} %y_ref.1, bf16[729,729]{1,0:T(8,128)(2,1)} %kin_ref.1, f32[4]{0:T(128)} %scale_ref.1, f32[4,729]{1,0:T(4,128)} %pot_ref.1, s32[4,729]{1,0:T(4,128)} %cn_ref.1, s32[2,289]{1,0:T(2,128)} %fs_ref.1, s32[2,153]{1,0:T(2,128)} %fl_ref.1, bf16[18,4,729]{2,1,0:T(4,128)(2,1)} %bitcast.2, ...), custom_call_target="tpu_custom_call" | custom-call | tf_op jit(solution)/shard_map/pallas_call | solution.py:409
  42.4 2.0 %copy.12 = f32[64,2601]{1,0:T(8,128)} copy(f32[64,2601]{1,0:T(8,128)} %shard_map.100) | data formatting | bytes 1331712

commit v2 on v1

--- a/solution.py
+++ b/solution.py
@@ -11,6 +11,7 @@
 filter_half = 8.0
 BLK = 256
 SHIFT = 8
+EDGE = 128
 MESH = pl.DeviceIdType.MESH
 NT = (((1,), (1,)), ((), ()))
 f32 = jnp.float32
@@ -50,16 +51,22 @@
     asm,
     field,
     outg,
-    in_space,
     in_slab,
     inc,
     marg,
+    pn,
+    ct,
+    spot,
+    edge_send,
+    in_edge,
     pack_send,
     pack_recv,
     marg_send,
     marg_recv,
     face_send,
     face_recv,
+    edge_sem,
+    edge_got,
 ):
     n_space, n_slab = dims["n_space"], dims["n_slab"]
     width, nodes, cells, order = dims["width"], dims["nodes"], dims["cells"], dims["order"]
@@ -77,6 +84,50 @@
     l = lax.axis_index("slab")
     above, below = lax.rem(s + 1, n_space), lax.rem(s + n_space - 1, n_space)
     right, left = lax.rem(l + 1, n_slab), lax.rem(l + n_slab - 1, n_slab)
+    to_space, to_slab = (below, above), (left, right)
+    has_space, has_slab = (s > 0, s < n_space - 1), (l > 0, l < n_slab - 1)
+    corners = [(a, b) for a in range(2) for b in range(2)]
+
+    barrier = pltpu.get_barrier_semaphore()
+
+    def greet(exists, device):
+        @pl.when(exists)
+        def _():
+            pl.semaphore_signal(barrier, inc=1, device_id=device, device_id_type=MESH)
+
+        return exists.astype(jnp.int32)
+
+    for d in range(1, n_slab):
+        pl.semaphore_signal(
+            barrier, inc=1, device_id={"slab": lax.rem(l + d, n_slab)}, device_id_type=MESH
+        )
+    greeted = n_slab - 1
+    for a in range(2):
+        greeted += greet(has_space[a], {"space": to_space[a]})
+    for a, b in corners:
+        greeted += greet(has_space[a] & has_slab[b], {"space": to_space[a], "slab": to_slab[b]})
+    for a in range(2):
+
+        @pl.when(jnp.logical_not(has_space[a]))
+        def _():
+            for step in range(2):
+                inc[step, :, a * fsp : (a + 1) * fsp] = jnp.zeros((width, fsp), bf16)
+
+        @pl.when(jnp.logical_not(has_slab[a]))
+        def _():
+            for step in range(2):
+                in_slab[step, a] = jnp.zeros((width, flp), bf16)
+
+    for a, b in corners:
+
+        @pl.when(jnp.logical_not(has_space[a] & has_slab[b]))
+        def _():
+            for step in range(2):
+                in_edge[step, b, :, a * EDGE : (a + 1) * EDGE] = jnp.zeros((width, EDGE), bf16)
+
+    if fp > 2 * fsp + 2 * flp:
+        for step in range(2):
+            inc[step, :, 2 * fsp + 2 * flp :] = jnp.zeros((width, fp - 2 * fsp - 2 * flp), bf16)
 
     lane_cell = lax.broadcasted_iota(jnp.int32, (8, lp), 1) // pstride
     atom_row = jnp.zeros((8, lp), f32)
@@ -91,15 +142,8 @@
         for c in range(1, cells):
             many = many + pltpu.roll(once, c * pstride, 1)
         pack[part, :] = many
-    pack[atoms * pstride :, :] = atom_row
-
-    barrier = pltpu.get_barrier_semaphore()
-    for d in range(1, n_slab):
-        pl.semaphore_signal(
-            barrier, inc=1, device_id={"slab": lax.rem(l + d, n_slab)}, device_id_type=MESH
-        )
-    for t in (above, below):
-        pl.semaphore_signal(barrier, inc=1, device_id={"space": t}, device_id_type=MESH)
+    pack[atoms * pstride : atoms * pstride + 8, :] = atom_row
+
     idx[...] = jnp.full(idx.shape, -1, jnp.int32)
     for c in range(cells):
         idx[0:1, c * op : c * op + order] = cn_ref[c : c + 1, :]
@@ -146,7 +190,7 @@
         left_side, right_side = [], []
         for value, at in pieces:
             high = (idx[0:1, at] >> SHIFT).astype(f32).astype(bf16)
-            high = jnp.broadcast_to(high, (width, BLK))
+            high = jnp.broadcast_to(high, value.shape)
             none = jnp.zeros((), bf16)
             left_side.append(
                 jnp.concatenate(
@@ -163,7 +207,7 @@
 
     per_cell = op // BLK
     tiles = cells * per_cell
-    group = 2 if tiles % 2 == 0 else 1
+    group = max(g for g in (1, 2, 4) if tiles % g == 0)
 
     def take_cells(source, build):
         def body(i):
@@ -187,7 +231,78 @@
         col = jnp.broadcast_to(row, (128, 128)).T
         cross[k * 128 : (k + 1) * 128, :] = jnp.where(col[:, 0:1] == slab_row, 1.0, 0.0).astype(bf16)
 
-    pl.semaphore_wait(barrier, n_slab + 1)
+    row_at = lax.broadcasted_iota(jnp.int32, (16, flp), 0)
+    counts = (lax.broadcasted_iota(jnp.int32, (16, flp), 1) + 1).astype(f32)
+    probe = jnp.where(row_at == 0, 1.0, jnp.where(row_at == 1, counts, 0.0)).astype(bf16)
+    row_of = lax.broadcasted_iota(jnp.int32, (16, fsp), 0)
+    member, place = [], []
+    for b in range(2):
+        seen = lax.dot_general(
+            probe, cross[:, b * flp : (b + 1) * flp], NT, preferred_element_type=f32
+        )
+        for a in range(2):
+            member.append(jnp.broadcast_to(seen[0:1, a * fsp : (a + 1) * fsp], (16, fsp)))
+            place.append(jnp.broadcast_to(seen[1:2, a * fsp : (a + 1) * fsp], (16, fsp)))
+    stacked = jnp.zeros((16, fsp), f32)
+    for i in range(4):
+        stacked = jnp.where(row_of == i, member[i], stacked)
+    tri_row = lax.broadcasted_iota(jnp.int32, (fsp, fsp), 0)
+    tri_col = lax.broadcasted_iota(jnp.int32, (fsp, fsp), 1)
+    before = jnp.where(tri_row < tri_col, 1.0, 0.0).astype(bf16)
+    rank = jnp.dot(stacked.astype(bf16), before, preferred_element_type=f32)
+    edge_row = lax.broadcasted_iota(jnp.int32, (EDGE, fsp), 0).astype(f32)
+    spots = jnp.zeros((8, lp), f32)
+    spot_row = lax.broadcasted_iota(jnp.int32, (8, EDGE), 0)
+    for i in range(4):
+        b, a = i // 2, i % 2
+        label = jnp.where(member[i][0:1] > 0.5, rank[i : i + 1], -1.0)
+        picked = jnp.where(edge_row == jnp.broadcast_to(label, (EDGE, fsp)), 1.0, 0.0).astype(bf16)
+        ct[a, b * EDGE : (b + 1) * EDGE, :] = picked
+        listed = lax.dot_general(place[i].astype(bf16), picked, NT, preferred_element_type=f32)
+        spots = jnp.where(spot_row == i, listed[0:8], spots)
+    pack[atoms * pstride + 8 :, :] = spots
+
+    pl.loop(0, tiles // group)(take_cells(yb, True))
+
+    def margin_of(step):
+        margin = jnp.zeros((width, lp), f32)
+        if step == 0:
+            for c in range(cells):
+                margin += lax.dot_general(
+                    vals[c * width : (c + 1) * width, :],
+                    pp[:, c * op : (c + 1) * op],
+                    NT,
+                    preferred_element_type=f32,
+                )
+        else:
+            for b in range(blocks):
+                margin += lax.dot_general(
+                    yb[b * width : (b + 1) * width, :],
+                    pn[b * lp : (b + 1) * lp, :],
+                    NT,
+                    preferred_element_type=f32,
+                )
+        marg[step, 0] = margin
+        return margin
+
+    def send_margin(step):
+        copies = []
+        for d in range(1, n_slab):
+            copy = pltpu.make_async_remote_copy(
+                src_ref=marg.at[step, 0],
+                dst_ref=marg.at[step, d],
+                send_sem=marg_send.at[step, d - 1],
+                recv_sem=marg_recv.at[step, d - 1],
+                device_id={"slab": lax.rem(l + d, n_slab)},
+                device_id_type=MESH,
+            )
+            copy.start()
+            copies.append(copy)
+        return copies
+
+    margin_of(0)
+    pl.semaphore_wait(barrier, greeted)
+    marg_copies = send_margin(0)
     pack_copies = []
     for d in range(1, n_slab):
         copy = pltpu.make_async_remote_copy(
@@ -201,88 +316,124 @@
         copy.start()
         pack_copies.append(copy)
 
-    pl.loop(0, tiles // group)(take_cells(yb, True))
-
-    for copy in pack_copies:
-        copy.wait()
-    own_row = pack[atoms * pstride : atoms * pstride + 1, :]
-    own_col = jnp.broadcast_to(own_row, (lp, lp)).T
-    chosen = jnp.zeros((lp, lp), f32)
-    for d in range(n_slab):
-        source = lax.rem(l + n_slab - d, n_slab)
-        for i in range(atoms):
-            part = slice(i * pstride, (i + 1) * pstride)
-            block = pack[part, :] if d == 0 else packs[d - 1, part, :]
-            tiled = jnp.concatenate([block] * cells, axis=0)
-            chosen += jnp.where(own_col == (source * atoms + i).astype(f32), tiled, 0.0)
-    for d in range(n_slab):
-        last = slice(atoms * pstride, atoms * pstride + 1)
-        row = pack[last, :] if d == 0 else packs[d - 1, last, :]
-        coup[d] = jnp.where(own_col == row, chosen, 0.0)
-
-    lanes = lax.broadcasted_iota(jnp.int32, (1, fp), 1)
-    has_below, has_above = s > 0, s < n_space - 1
-    has_left, has_right = l > 0, l < n_slab - 1
-    keep = (
-        ((lanes < fsp) & has_below)
-        | ((lanes >= fsp) & (lanes < o_sl) & has_above)
-        | ((lanes >= o_sl) & (lanes < o_sl + flp) & has_left)
-        | ((lanes >= o_sl + flp) & (lanes < o_sl + 2 * flp) & has_right)
-    ).astype(f32)
-
-    inc[...] = jnp.zeros(inc.shape, bf16)
-
-    def face_copy(step, which, src, landing, device):
-        count = landing.shape[-1]
-        return pltpu.make_async_remote_copy(
-            src_ref=outg.at[step, :, src : src + count],
-            dst_ref=landing.at[step, which % 2],
-            send_sem=face_send.at[step, which],
-            recv_sem=face_recv.at[step, which],
-            device_id=device,
-            device_id_type=MESH,
-        )
+    def use_packs():
+        for copy in pack_copies:
+            copy.wait()
+        own_row = pack[atoms * pstride : atoms * pstride + 1, :]
+        own_col = jnp.broadcast_to(own_row, (lp, lp)).T
+        chosen = jnp.zeros((lp, lp), f32)
+        for d in range(n_slab):
+            source = lax.rem(l + n_slab - d, n_slab)
+            for i in range(atoms):
+                part = slice(i * pstride, (i + 1) * pstride)
+                block = pack[part, :] if d == 0 else packs[d - 1, part, :]
+                tiled = jnp.concatenate([block] * cells, axis=0)
+                chosen += jnp.where(own_col == (source * atoms + i).astype(f32), tiled, 0.0)
+        for d in range(n_slab):
+            last = slice(atoms * pstride, atoms * pstride + 1)
+            row = pack[last, :] if d == 0 else packs[d - 1, last, :]
+            coup[d] = jnp.where(own_col == row, chosen, 0.0)
+        slot = lax.broadcasted_iota(jnp.int32, (flp, EDGE), 0).astype(f32) + 1.0
+        for b in range(2):
+            d = 1 if b == 0 else n_slab - 1
+            for a in range(2):
+                at = atoms * pstride + 8 + (1 - b) * 2 + a
+                row = packs[max(d - 1, 0), at : at + 1, 0:EDGE]
+                spot[b, :, a * EDGE : (a + 1) * EDGE] = jnp.where(
+                    slot == jnp.broadcast_to(row, (flp, EDGE)), 1.0, 0.0
+                ).astype(bf16)
+
+    def place_projectors():
+        @pl.loop(0, cells)
+        def _(c):
+            row = pl.ds(pl.multiple_of(c * pstride, pstride), pstride)
+            placed = spread(
+                [(pp[row, tile(c * op + n * BLK)], tile(c * op + n * BLK)) for n in range(per_cell)]
+            ).astype(bf16)
+            for b in range(blocks):
+                to = pl.ds(pl.multiple_of(b * lp + c * pstride, pstride), pstride)
+                pn[to, :] = placed[b * pstride : (b + 1) * pstride]
+
+    def exchange(step):
+        moves = []
+
+        def move(sends, gets, source, target, out_sem, in_sem, device):
+            copy = pltpu.make_async_remote_copy(
+                src_ref=source,
+                dst_ref=target,
+                send_sem=out_sem,
+                recv_sem=in_sem,
+                device_id=device,
+                device_id_type=MESH,
+            )
+            pl.when(sends)(copy.start)
+            moves.append((sends, gets, copy))
+
+        cut = up(o_sl, BLK)
+        take_faces(step, 0, cut)
+        for a in range(2):
+            seg = slice(a * fsp, (a + 1) * fsp)
+            other = slice((1 - a) * fsp, (2 - a) * fsp)
+            move(
+                has_space[a],
+                has_space[1 - a],
+                outg.at[step, :, seg],
+                inc.at[step, :, other],
+                face_send.at[step, a],
+                face_recv.at[step, a],
+                {"space": to_space[a]},
+            )
+        for a in range(2):
+            edge_send[step, a] = lax.dot_general(
+                outg[step, :, a * fsp : (a + 1) * fsp], ct[a], NT, preferred_element_type=f32
+            ).astype(bf16)
+        for a, b in corners:
+            move(
+                has_space[a] & has_slab[b],
+                has_space[1 - a] & has_slab[1 - b],
+                edge_send.at[step, a, :, b * EDGE : (b + 1) * EDGE],
+                in_edge.at[step, 1 - b, :, (1 - a) * EDGE : (2 - a) * EDGE],
+                edge_sem.at[step, 2 * a + b],
+                edge_got.at[step, 2 * a + b],
+                {"space": to_space[a], "slab": to_slab[b]},
+            )
+        take_faces(step, cut, fp)
+        for b in range(2):
+            move(
+                has_slab[b],
+                has_slab[1 - b],
+                outg.at[step, :, o_sl + b * flp : o_sl + (b + 1) * flp],
+                in_slab.at[step, 1 - b],
+                face_send.at[step, 2 + b],
+                face_recv.at[step, 2 + b],
+                {"slab": to_slab[b]},
+            )
+        return moves
+
+    def finish(step, moves):
+        for sends, gets, copy in moves:
+            pl.when(gets)(copy.wait_recv)
+        for sends, gets, copy in moves:
+            pl.when(sends)(copy.wait_send)
+        for b in range(2):
+            part = slice(o_sl + b * flp, o_sl + (b + 1) * flp)
+            corner = lax.dot_general(in_edge[step, b], spot[b], NT, preferred_element_type=f32)
+            inc[step, :, part] = (in_slab[step, b].astype(f32) + corner).astype(bf16)
+        return spread([(inc[step, :, tile(k * BLK)], tile(jp + k * BLK)) for k in range(fp // BLK)])
+
+    def take_faces(step, first, last):
+        for k in range(first // BLK, last // BLK):
+            outg[step, :, tile(k * BLK)] = gather(yb, tile(jp + k * BLK))
 
     for step in range(2):
         if step == 1:
+            margin_of(1)
+            marg_copies = send_margin(1)
             pl.loop(0, tiles // group)(take_cells(yb, False))
-        margin = jnp.zeros((width, lp), f32)
+        kinv[...] = jnp.dot(vals[...], kin[...], preferred_element_type=f32)
         for c in range(cells):
-            margin += lax.dot_general(
-                vals[c * width : (c + 1) * width, :],
-                pp[:, c * op : (c + 1) * op],
-                NT,
-                preferred_element_type=f32,
-            )
-        marg[step, 0] = margin
-        marg_copies = []
-        for d in range(1, n_slab):
-            copy = pltpu.make_async_remote_copy(
-                src_ref=marg.at[step, 0],
-                dst_ref=marg.at[step, d],
-                send_sem=marg_send.at[step, d - 1],
-                recv_sem=marg_recv.at[step, d - 1],
-                device_id={"slab": lax.rem(l + d, n_slab)},
-                device_id_type=MESH,
-            )
-            copy.start()
-            marg_copies.append(copy)
-
-        kinv[...] = jnp.dot(vals[...], kin[...], preferred_element_type=f32)
-        coupled = lax.dot_general(
-            margin, coup[0], NT, precision=lax.Precision.HIGHEST, preferred_element_type=f32
-        )
-        for d in range(1, n_slab):
-            marg_copies[d - 1].wait()
-            coupled += lax.dot_general(
-                marg[step, d], coup[d], NT, precision=lax.Precision.HIGHEST, preferred_element_type=f32
-            )
-        coupled = coupled.astype(bf16)
-        for c in range(cells):
-            cols = slice(c * op, (c + 1) * op)
             rows = slice(c * width, (c + 1) * width)
-            total = jnp.dot(coupled, pp[:, cols], preferred_element_type=f32)
-            total += scale_ref[c] * kinv[rows, :] + pot[c : c + 1, :] * vals[rows, :].astype(f32)
+            total = scale_ref[c] * kinv[rows, :] + pot[c : c + 1, :] * vals[rows, :].astype(f32)
             tot[rows, :] = total.astype(bf16)
 
         asm[...] = jnp.zeros(asm.shape, f32)
@@ -294,21 +445,26 @@
                 [(tot[row, tile(n * BLK)], tile(c * op + n * BLK)) for n in range(per_cell)]
             )
 
-        yb[...] = asm[...].astype(bf16)
-
-        def take_faces(first, last):
-            for k in range(first // BLK, last // BLK):
-                outg[step, :, tile(k * BLK)] = gather(yb, tile(jp + k * BLK))
-
-        cut = up(o_sl, BLK)
-        take_faces(0, cut)
-        space_copies = [
-            face_copy(step, 0, fsp, in_space, {"space": above}),
-            face_copy(step, 1, 0, in_space, {"space": below}),
-        ]
-        for copy in space_copies:
-            copy.start()
-        take_faces(cut, fp)
+        if step == 0:
+            place_projectors()
+            use_packs()
+        coupled = jnp.zeros((width, lp), f32)
+        for d in range(n_slab):
+            if d > 0:
+                marg_copies[d - 1].wait()
+            coupled += lax.dot_general(
+                marg[step, d], coup[d], NT, precision=lax.Precision.HIGHEST, preferred_element_type=f32
+            )
+        coupled = coupled.astype(bf16)
+        for b in range(blocks):
+            rows = slice(b * width, (b + 1) * width)
+            whole = asm[rows, :] + jnp.dot(
+                coupled, pn[b * lp : (b + 1) * lp, :], preferred_element_type=f32
+            )
+            asm[rows, :] = whole
+            yb[rows, :] = whole.astype(bf16)
+
+        moves = exchange(step)
 
         if step == 0:
             for b in range(blocks):
@@ -319,6 +475,9 @@
                 ].astype(f32)
                 if count < BLK:
                     field[rows, count:] = jnp.zeros((width, BLK - count), f32)
+            fresh = (field[...] + finish(step, moves)) / filter_half
+            field[...] = fresh
+            yb[...] = fresh.astype(bf16)
         else:
             for b in range(blocks):
                 rows = slice(b * width, (b + 1) * width)
@@ -329,48 +488,13 @@
                     - 2.0 * filter_centre / filter_half * field[rows, 0:count]
                     - start
                 )
-
-        for k, copy in enumerate(space_copies):
-            copy.wait()
-            part = slice(k * fsp, (k + 1) * fsp)
-            inc[step, :, part] = (in_space[step, k].astype(f32) * keep[:, part]).astype(bf16)
-        extra = jnp.dot(inc[step, :, 0:o_sl], cross[...], preferred_element_type=f32)
-        part = slice(o_sl, o_sl + 2 * flp)
-        outg[step, :, part] = (outg[step, :, part].astype(f32) + extra).astype(bf16)
-        slab_copies = [
-            face_copy(step, 2, o_sl + flp, in_slab, {"slab": right}),
-            face_copy(step, 3, o_sl, in_slab, {"slab": left}),
-        ]
-        for copy in slab_copies:
-            copy.start()
-
-        def add_faces(first, last):
-            return spread(
-                [
-                    (inc[step, :, tile(k * BLK)], tile(jp + k * BLK))
-                    for k in range(first // BLK, last // BLK)
-                ]
-            )
-
-        whole = o_sl // BLK * BLK
-        gain = 1.0 if step == 0 else 2.0 / filter_half
-        into = field if step == 0 else asm
-        if whole:
-            into[...] += gain * add_faces(0, whole)
-
-        for k, copy in enumerate(slab_copies):
-            copy.wait()
-            part = slice(o_sl + k * flp, o_sl + (k + 1) * flp)
-            inc[step, :, part] = (in_slab[step, k].astype(f32) * keep[:, part]).astype(bf16)
-        rest = into[...] + gain * add_faces(whole, fp)
-        if step == 0:
-            rest = rest / filter_half
-            field[...] = rest
-            yb[...] = rest.astype(bf16)
-        else:
+            added = finish(step, moves)
             for b in range(blocks):
+                rows = slice(b * width, (b + 1) * width)
                 count = min(BLK, nodes - b * BLK)
-                out_ref[:, b * BLK : b * BLK + count] = rest[b * width : (b + 1) * width, 0:count]
+                out_ref[:, b * BLK : b * BLK + count] = (
+                    asm[rows, 0:count] + 2.0 / filter_half * added[rows, 0:count]
+                )
 
 
 def shards(
@@ -413,13 +537,13 @@
         out_specs=vmem,
         scratch_shapes=[
             pltpu.VMEM((BLK, jp + fp), bf16),
-            pltpu.VMEM((atoms * pstride + 8, lp), f32),
+            pltpu.VMEM((atoms * pstride + 16, lp), f32),
             pltpu.VMEM((8, jp + fp), jnp.int32),
             pltpu.VMEM((op, op), bf16),
             pltpu.VMEM((lp, jp), bf16),
             pltpu.VMEM((up(cells, 8), op), f32),
             pltpu.VMEM((2 * fsp, 2 * flp), bf16),
-            pltpu.VMEM((others, atoms * pstride + 8, lp), f32),
+            pltpu.VMEM((others, atoms * pstride + 16, lp), f32),
             pltpu.VMEM((n_slab, lp, lp), f32),
             pltpu.VMEM((npad // BLK * width, BLK), bf16),
             pltpu.VMEM((cells * width, op), bf16),
@@ -428,14 +552,20 @@
             pltpu.VMEM((npad // BLK * width, BLK), f32),
             pltpu.VMEM((npad // BLK * width, BLK), f32),
             pltpu.VMEM((2, width, fp), bf16),
-            pltpu.VMEM((2, 2, width, fsp), bf16),
             pltpu.VMEM((2, 2, width, flp), bf16),
             pltpu.VMEM((2, width, fp), bf16),
             pltpu.VMEM((2, n_slab, width, lp), f32),
+            pltpu.VMEM((npad // BLK * lp, BLK), bf16),
+            pltpu.VMEM((2, 2 * EDGE, fsp), bf16),
+            pltpu.VMEM((2, flp, 2 * EDGE), bf16),
+            pltpu.VMEM((2, 2, width, 2 * EDGE), bf16),
+            pltpu.VMEM((2, 2, width, 2 * EDGE), bf16),
             dma((others,)),
             dma((others,)),
             dma((2, others)),
             dma((2, others)),
+            dma((2, 4)),
+            dma((2, 4)),
             dma((2, 4)),
             dma((2, 4)),
         ],

time: 44.5 us -> 30.7 us (0.69)
  Pallas kernels: 42.4 us -> 28.5 us
    pallas_call x1, Pallas kernels: 42.4 us -> 28.5 us  [shards(): pl.pallas_call(functools.partial(kernel, dims), out_shape=jax.ShapeDtypeS...]
where the time goes in v2:
time: 30.7 us; the launch traced here: 30.5 us
  Pallas kernels  28.5 us (93%)
  local copies, waits for them, and re-layouts  1.99 us (6%)
    pallas_call x1, Pallas kernels, shards(): pl.pallas_call(functools.partial(kernel, dims), out_shape=jax.ShapeDtypeS...  28.5 us
    unnamed x1, local copies, waits for them, and re-layouts  1.99 us

profile of v2, /device:TPU:0, one launch (start us, length us, event | category | flops | bytes accessed | tf_op | source)
XLA Modules:
  0.0 30.5 jit_solution(16385065610622592249)
XLA Ops:
  0.0 28.5 %shard_map.100 = f32[64,2601]{1,0:T(8,128)} custom-call(bf16[64,2601]{1,0:T(8,128)(2,1)} %y_ref.1, bf16[729,729]{1,0:T(8,128)(2,1)} %kin_ref.1, f32[4]{0:T(128)} %scale_ref.1, f32[4,729]{1,0:T(4,128)} %pot_ref.1, s32[4,729]{1,0:T(4,128)} %cn_ref.1, s32[2,289]{1,0:T(2,128)} %fs_ref.1, s32[2,153]{1,0:T(2,128)} %fl_ref.1, bf16[18,4,729]{2,1,0:T(4,128)(2,1)} %bitcast.2, ...), custom_call_target="tpu_custom_call" | custom-call | tf_op jit(solution)/shard_map/pallas_call | solution.py:533
  28.5 2.0 %copy.12 = f32[64,2601]{1,0:T(8,128)} copy(f32[64,2601]{1,0:T(8,128)} %shard_map.100) | data formatting | bytes 1331712

commit v3 on v2

--- a/solution.py
+++ b/solution.py
@@ -24,6 +24,17 @@
 
 def kernel(
     dims,
+    y_hbm,
+    kin_hbm,
+    scale_hbm,
+    pot_hbm,
+    cn_hbm,
+    fs_hbm,
+    fl_hbm,
+    pr_hbm,
+    atom_hbm,
+    coupling_hbm,
+    out_ref,
     y_ref,
     kin_ref,
     scale_ref,
@@ -34,7 +45,7 @@
     pr_ref,
     atom_ref,
     coupling_ref,
-    out_ref,
+    in_sem,
     hot,
     pack,
     idx,
@@ -78,7 +89,20 @@
     fp = up(2 * fsp + 2 * flp, BLK)
     lp = cells * pstride
     o_sl = 2 * fsp
+    wide = up(max(atoms * pstride, lp, EDGE), 128)
     blocks = npad // BLK
+
+    outside = (
+        y_hbm, kin_hbm, scale_hbm, pot_hbm, cn_hbm, fs_hbm, fl_hbm, pr_hbm, atom_hbm, coupling_hbm
+    )
+    inside = (
+        y_ref, kin_ref, scale_ref, pot_ref, cn_ref, fs_ref, fl_ref, pr_ref, atom_ref, coupling_ref
+    )
+    loads = [
+        pltpu.make_async_copy(outside[i], inside[i], in_sem.at[i]) for i in range(len(outside))
+    ]
+    for i in (4, 5, 6, 0, 8, 9, 7, 1, 2, 3):
+        loads[i].start()
 
     s = lax.axis_index("space")
     l = lax.axis_index("slab")
@@ -129,21 +153,8 @@
         for step in range(2):
             inc[step, :, 2 * fsp + 2 * flp :] = jnp.zeros((width, fp - 2 * fsp - 2 * flp), bf16)
 
-    lane_cell = lax.broadcasted_iota(jnp.int32, (8, lp), 1) // pstride
-    atom_row = jnp.zeros((8, lp), f32)
-    for c in range(cells):
-        atom_row = jnp.where(lane_cell == c, atom_ref[c].astype(f32), atom_row)
-    pack[...] = jnp.zeros(pack.shape, f32)
-    for i in range(atoms):
-        part = slice(i * pstride, (i + 1) * pstride)
-        pack[i * pstride : i * pstride + nproj, 0:nproj] = coupling_ref[:, i, :]
-        once = pack[part, :]
-        many = once
-        for c in range(1, cells):
-            many = many + pltpu.roll(once, c * pstride, 1)
-        pack[part, :] = many
-    pack[atoms * pstride : atoms * pstride + 8, :] = atom_row
-
+    for i in (4, 5, 6):
+        loads[i].wait()
     idx[...] = jnp.full(idx.shape, -1, jnp.int32)
     for c in range(cells):
         idx[0:1, c * op : c * op + order] = cn_ref[c : c + 1, :]
@@ -152,20 +163,13 @@
         off = jp + o_sl + k * flp
         idx[0:1, off : off + fl] = fl_ref[k : k + 1, :]
 
+    loads[0].wait()
     for b in range(blocks):
         count = min(BLK, nodes - b * BLK)
         rows = slice(b * width, (b + 1) * width)
         if count < BLK:
             yb[rows, :] = jnp.zeros((width, BLK), bf16)
         yb[rows, 0:count] = y_ref[:, b * BLK : b * BLK + count]
-    kin[...] = jnp.zeros(kin.shape, bf16)
-    kin[0:order, 0:order] = kin_ref[...]
-    pp[...] = jnp.zeros(pp.shape, bf16)
-    pot[...] = jnp.zeros(pot.shape, f32)
-    pot[0:cells, 0:order] = pot_ref[...]
-    for c in range(cells):
-        pp[c * pstride : c * pstride + nproj, c * op : c * op + order] = pr_ref[:, c, :]
-
     lane_rows = lax.broadcasted_iota(jnp.int32, (BLK, BLK), 0).astype(f32).astype(bf16)
 
     def tile(start):
@@ -231,6 +235,26 @@
         col = jnp.broadcast_to(row, (128, 128)).T
         cross[k * 128 : (k + 1) * 128, :] = jnp.where(col[:, 0:1] == slab_row, 1.0, 0.0).astype(bf16)
 
+    loads[8].wait()
+    loads[9].wait()
+    lane_cell = lax.broadcasted_iota(jnp.int32, (8, lp), 1) // pstride
+    atom_row = jnp.zeros((8, lp), f32)
+    for c in range(cells):
+        atom_row = jnp.where(lane_cell == c, atom_ref[c].astype(f32), atom_row)
+    pack[...] = jnp.zeros(pack.shape, f32)
+    for i in range(atoms):
+        pack[0:nproj, i * pstride : i * pstride + nproj] = coupling_ref[:, i, :]
+    pack[pstride : pstride + 8, 0:lp] = atom_row
+    loads[7].wait()
+    pp[...] = jnp.zeros(pp.shape, bf16)
+    for c in range(cells):
+        pp[c * pstride : c * pstride + nproj, c * op : c * op + order] = pr_ref[:, c, :]
+    for i in (1, 2, 3):
+        loads[i].wait()
+    kin[...] = jnp.zeros(kin.shape, bf16)
+    kin[0:order, 0:order] = kin_ref[...]
+    pot[...] = jnp.zeros(pot.shape, f32)
+    pot[0:cells, 0:order] = pot_ref[...]
     row_at = lax.broadcasted_iota(jnp.int32, (16, flp), 0)
     counts = (lax.broadcasted_iota(jnp.int32, (16, flp), 1) + 1).astype(f32)
     probe = jnp.where(row_at == 0, 1.0, jnp.where(row_at == 1, counts, 0.0)).astype(bf16)
@@ -251,7 +275,7 @@
     before = jnp.where(tri_row < tri_col, 1.0, 0.0).astype(bf16)
     rank = jnp.dot(stacked.astype(bf16), before, preferred_element_type=f32)
     edge_row = lax.broadcasted_iota(jnp.int32, (EDGE, fsp), 0).astype(f32)
-    spots = jnp.zeros((8, lp), f32)
+    spots = jnp.zeros((8, EDGE), f32)
     spot_row = lax.broadcasted_iota(jnp.int32, (8, EDGE), 0)
     for i in range(4):
         b, a = i // 2, i % 2
@@ -260,7 +284,7 @@
         ct[a, b * EDGE : (b + 1) * EDGE, :] = picked
         listed = lax.dot_general(place[i].astype(bf16), picked, NT, preferred_element_type=f32)
         spots = jnp.where(spot_row == i, listed[0:8], spots)
-    pack[atoms * pstride + 8 :, :] = spots
+    pack[pstride + 8 :, 0:EDGE] = spots
 
     pl.loop(0, tiles // group)(take_cells(yb, True))
 
@@ -300,7 +324,53 @@
             copies.append(copy)
         return copies
 
+    def place_projectors(first, last):
+        @pl.loop(first, last)
+        def _(c):
+            row = pl.ds(pl.multiple_of(c * pstride, pstride), pstride)
+            placed = spread(
+                [(pp[row, tile(c * op + n * BLK)], tile(c * op + n * BLK)) for n in range(per_cell)]
+            ).astype(bf16)
+            for b in range(blocks):
+                to = pl.ds(pl.multiple_of(b * lp + c * pstride, pstride), pstride)
+                pn[to, :] = placed[b * pstride : (b + 1) * pstride]
+
+    def local_part():
+        kinv[...] = jnp.dot(vals[...], kin[...], preferred_element_type=f32)
+        for c in range(cells):
+            rows = slice(c * width, (c + 1) * width)
+            total = scale_ref[c] * kinv[rows, :] + pot[c : c + 1, :] * vals[rows, :].astype(f32)
+            tot[rows, :] = total.astype(bf16)
+
+    span = 1
+
+    def scatter():
+        def some(first):
+            return spread(
+                [
+                    (tot[rows_of(first, c), tile(n * BLK)], tile((first + c) * op + n * BLK))
+                    for c in range(span)
+                    for n in range(per_cell)
+                ]
+            )
+
+        def rows_of(first, c):
+            start = (first + c) * width
+            if isinstance(start, int):
+                return slice(start, start + width)
+            return pl.ds(pl.multiple_of(start, width), width)
+
+        asm[...] = some(0)
+        if cells > span:
+
+            @pl.loop(1, cells // span)
+            def _(i):
+                asm[...] += some(i * span)
+
     margin_of(0)
+    local_part()
+    early = 0
+    place_projectors(0, early)
     pl.semaphore_wait(barrier, greeted)
     marg_copies = send_margin(0)
     pack_copies = []
@@ -319,40 +389,34 @@
     def use_packs():
         for copy in pack_copies:
             copy.wait()
-        own_row = pack[atoms * pstride : atoms * pstride + 1, :]
+        own_row = pack[pstride : pstride + 1, 0:lp]
         own_col = jnp.broadcast_to(own_row, (lp, lp)).T
+        segment = lax.broadcasted_iota(jnp.int32, (pstride, wide), 1) // pstride
         chosen = jnp.zeros((lp, lp), f32)
         for d in range(n_slab):
             source = lax.rem(l + n_slab - d, n_slab)
+            table = pack[0:pstride, :] if d == 0 else packs[d - 1, 0:pstride, :]
             for i in range(atoms):
-                part = slice(i * pstride, (i + 1) * pstride)
-                block = pack[part, :] if d == 0 else packs[d - 1, part, :]
-                tiled = jnp.concatenate([block] * cells, axis=0)
+                once = jnp.where(segment == i, table, 0.0)
+                many = once
+                for c in range(cells):
+                    if c != i:
+                        many = many + pltpu.roll(once, (c - i) * pstride % wide, 1)
+                tiled = jnp.concatenate([many[:, 0:lp]] * cells, axis=0)
                 chosen += jnp.where(own_col == (source * atoms + i).astype(f32), tiled, 0.0)
         for d in range(n_slab):
-            last = slice(atoms * pstride, atoms * pstride + 1)
-            row = pack[last, :] if d == 0 else packs[d - 1, last, :]
+            last = slice(pstride, pstride + 1)
+            row = pack[last, 0:lp] if d == 0 else packs[d - 1, last, 0:lp]
             coup[d] = jnp.where(own_col == row, chosen, 0.0)
         slot = lax.broadcasted_iota(jnp.int32, (flp, EDGE), 0).astype(f32) + 1.0
         for b in range(2):
             d = 1 if b == 0 else n_slab - 1
             for a in range(2):
-                at = atoms * pstride + 8 + (1 - b) * 2 + a
+                at = pstride + 8 + (1 - b) * 2 + a
                 row = packs[max(d - 1, 0), at : at + 1, 0:EDGE]
                 spot[b, :, a * EDGE : (a + 1) * EDGE] = jnp.where(
                     slot == jnp.broadcast_to(row, (flp, EDGE)), 1.0, 0.0
                 ).astype(bf16)
-
-    def place_projectors():
-        @pl.loop(0, cells)
-        def _(c):
-            row = pl.ds(pl.multiple_of(c * pstride, pstride), pstride)
-            placed = spread(
-                [(pp[row, tile(c * op + n * BLK)], tile(c * op + n * BLK)) for n in range(per_cell)]
-            ).astype(bf16)
-            for b in range(blocks):
-                to = pl.ds(pl.multiple_of(b * lp + c * pstride, pstride), pstride)
-                pn[to, :] = placed[b * pstride : (b + 1) * pstride]
 
     def exchange(step):
         moves = []
@@ -430,23 +494,11 @@
             margin_of(1)
             marg_copies = send_margin(1)
             pl.loop(0, tiles // group)(take_cells(yb, False))
-        kinv[...] = jnp.dot(vals[...], kin[...], preferred_element_type=f32)
-        for c in range(cells):
-            rows = slice(c * width, (c + 1) * width)
-            total = scale_ref[c] * kinv[rows, :] + pot[c : c + 1, :] * vals[rows, :].astype(f32)
-            tot[rows, :] = total.astype(bf16)
-
-        asm[...] = jnp.zeros(asm.shape, f32)
-
-        @pl.loop(0, cells)
-        def _(c):
-            row = pl.ds(pl.multiple_of(c * width, width), width)
-            asm[...] += spread(
-                [(tot[row, tile(n * BLK)], tile(c * op + n * BLK)) for n in range(per_cell)]
-            )
+            local_part()
+        scatter()
 
         if step == 0:
-            place_projectors()
+            place_projectors(early, cells)
             use_packs()
         coupled = jnp.zeros((width, lp), f32)
         for d in range(n_slab):
@@ -527,23 +579,34 @@
     fp = up(2 * fsp + 2 * flp, BLK)
     lp = cells * pstride
     others = max(n_slab - 1, 1)
+    wide = up(max(atoms * pstride, lp, EDGE), 128)
     vmem = pl.BlockSpec(memory_space=pltpu.VMEM)
-    smem = pl.BlockSpec(memory_space=pltpu.SMEM)
     dma = pltpu.SemaphoreType.DMA
     return pl.pallas_call(
         functools.partial(kernel, dims),
-        out_shape=jax.ShapeDtypeStruct((width, nodes), f32),
-        in_specs=[vmem, vmem, smem] + [vmem] * 5 + [smem, vmem],
+        out_shape=pltpu.VMEM((width, nodes), f32),
+        in_specs=[pl.BlockSpec(memory_space=pl.ANY)] * 10,
         out_specs=vmem,
         scratch_shapes=[
+            pltpu.VMEM((width, nodes), bf16),
+            pltpu.VMEM((order, order), bf16),
+            pltpu.SMEM((cells,), f32),
+            pltpu.VMEM((cells, order), f32),
+            pltpu.VMEM((cells, order), jnp.int32),
+            pltpu.VMEM((2, fs), jnp.int32),
+            pltpu.VMEM((2, fl), jnp.int32),
+            pltpu.VMEM((nproj, cells, order), bf16),
+            pltpu.SMEM((cells,), jnp.int32),
+            pltpu.VMEM((nproj, atoms, nproj), f32),
+            dma((10,)),
             pltpu.VMEM((BLK, jp + fp), bf16),
-            pltpu.VMEM((atoms * pstride + 16, lp), f32),
+            pltpu.VMEM((pstride + 16, wide), f32),
             pltpu.VMEM((8, jp + fp), jnp.int32),
             pltpu.VMEM((op, op), bf16),
             pltpu.VMEM((lp, jp), bf16),
             pltpu.VMEM((up(cells, 8), op), f32),
             pltpu.VMEM((2 * fsp, 2 * flp), bf16),
-            pltpu.VMEM((others, atoms * pstride + 16, lp), f32),
+            pltpu.VMEM((others, pstride + 16, wide), f32),
             pltpu.VMEM((n_slab, lp, lp), f32),
             pltpu.VMEM((npad // BLK * width, BLK), bf16),
             pltpu.VMEM((cells * width, op), bf16),

time: 30.7 us -> 28.1 us (0.915)
  Pallas kernels: 28.5 us -> 27 us
  local copies, waits for them, and re-layouts: 1.99 us -> 0.85 us
    pallas_call x1, Pallas kernels: 28.5 us -> 27 us  [shards(): pl.pallas_call(functools.partial(kernel, dims), out_shape=pltpu.VMEM((wid...]
    unnamed x1, local copies, waits for them, and re-layouts: 1.99 us -> 0.85 us
where the time goes in v3:
time: 28.1 us; the launch traced here: 27.9 us
  Pallas kernels  27 us (96%)
  local copies, waits for them, and re-layouts  0.85 us (3%)
    pallas_call x1, Pallas kernels, shards(): pl.pallas_call(functools.partial(kernel, dims), out_shape=pltpu.VMEM((wid...  27 us
    unnamed x1, local copies, waits for them, and re-layouts  0.85 us

profile of v3, /device:TPU:0, one launch (start us, length us, event | category | flops | bytes accessed | tf_op | source)
XLA Modules:
  0.0 27.9 jit_solution(16739116211431707829)
XLA Ops:
  0.0 27.0 %shard_map.100 = f32[64,2601]{1,0:T(8,128)S(1)} custom-call(bf16[64,2601]{1,0:T(8,128)(2,1)} %y_hbm.1, bf16[729,729]{1,0:T(8,128)(2,1)} %kin_hbm.1, f32[4]{0:T(128)} %scale_hbm.1, f32[4,729]{1,0:T(4,128)} %pot_hbm.1, s32[4,729]{1,0:T(4,128)} %cn_hbm.1, s32[2,289]{1,0:T(2,128)} %fs_hbm.1, s32[2,153]{1,0:T(2,128)} %fl_hbm.1, bf16[18,4,729]{2,1,0:T(4,128)(2,1)} %bitcast.2, ...), custom_call_target="tpu_custom_call" | custom-call | tf_op jit(solution)/shard_map/pallas_call | solution.py:585
  27.0 0.8 %copy.12 = f32[64,2601]{1,0:T(8,128)} copy(f32[64,2601]{1,0:T(8,128)S(1)} %shard_map.100) | data formatting | bytes 1331712

commit v4 on v3

--- a/solution.py
+++ b/solution.py
@@ -286,7 +286,22 @@
         spots = jnp.where(spot_row == i, listed[0:8], spots)
     pack[pstride + 8 :, 0:EDGE] = spots
 
-    pl.loop(0, tiles // group)(take_cells(yb, True))
+    pl.loop(0, 1)(take_cells(yb, True))
+    pl.semaphore_wait(barrier, greeted)
+    pack_copies = []
+    for d in range(1, n_slab):
+        copy = pltpu.make_async_remote_copy(
+            src_ref=pack,
+            dst_ref=packs.at[d - 1],
+            send_sem=pack_send.at[d - 1],
+            recv_sem=pack_recv.at[d - 1],
+            device_id={"slab": lax.rem(l + d, n_slab)},
+            device_id_type=MESH,
+        )
+        copy.start()
+        pack_copies.append(copy)
+
+    pl.loop(1, tiles // group)(take_cells(yb, True))
 
     def margin_of(step):
         margin = jnp.zeros((width, lp), f32)
@@ -324,17 +339,6 @@
             copies.append(copy)
         return copies
 
-    def place_projectors(first, last):
-        @pl.loop(first, last)
-        def _(c):
-            row = pl.ds(pl.multiple_of(c * pstride, pstride), pstride)
-            placed = spread(
-                [(pp[row, tile(c * op + n * BLK)], tile(c * op + n * BLK)) for n in range(per_cell)]
-            ).astype(bf16)
-            for b in range(blocks):
-                to = pl.ds(pl.multiple_of(b * lp + c * pstride, pstride), pstride)
-                pn[to, :] = placed[b * pstride : (b + 1) * pstride]
-
     def local_part():
         kinv[...] = jnp.dot(vals[...], kin[...], preferred_element_type=f32)
         for c in range(cells):
@@ -342,50 +346,36 @@
             total = scale_ref[c] * kinv[rows, :] + pot[c : c + 1, :] * vals[rows, :].astype(f32)
             tot[rows, :] = total.astype(bf16)
 
-    span = 1
-
-    def scatter():
-        def some(first):
-            return spread(
-                [
-                    (tot[rows_of(first, c), tile(n * BLK)], tile((first + c) * op + n * BLK))
-                    for c in range(span)
-                    for n in range(per_cell)
-                ]
-            )
-
-        def rows_of(first, c):
-            start = (first + c) * width
-            if isinstance(start, int):
-                return slice(start, start + width)
-            return pl.ds(pl.multiple_of(start, width), width)
-
-        asm[...] = some(0)
-        if cells > span:
-
-            @pl.loop(1, cells // span)
-            def _(i):
-                asm[...] += some(i * span)
+    def scatter(step):
+        def one(c, fresh):
+            row = c * width if isinstance(c, int) else pl.multiple_of(c * width, width)
+            low = c * pstride if isinstance(c, int) else pl.multiple_of(c * pstride, pstride)
+            pieces = []
+            for n in range(per_cell):
+                at = tile(c * op + n * BLK)
+                value = tot[pl.ds(row, width), tile(n * BLK)]
+                if step == 0:
+                    value = jnp.concatenate([value, pp[pl.ds(low, pstride), at]], axis=0)
+                pieces.append((value, at))
+            result = spread(pieces)
+            each = width if step else width + pstride
+            for b in range(blocks):
+                rows = slice(b * width, (b + 1) * width)
+                part = result[b * each : b * each + width]
+                asm[rows, :] = part if fresh else asm[rows, :] + part
+                if step == 0:
+                    to = pl.ds(b * lp + low, pstride)
+                    pn[to, :] = result[b * each + width : (b + 1) * each].astype(bf16)
+
+        one(0, True)
+
+        @pl.loop(1, cells)
+        def _(c):
+            one(c, False)
 
     margin_of(0)
+    marg_copies = send_margin(0)
     local_part()
-    early = 0
-    place_projectors(0, early)
-    pl.semaphore_wait(barrier, greeted)
-    marg_copies = send_margin(0)
-    pack_copies = []
-    for d in range(1, n_slab):
-        copy = pltpu.make_async_remote_copy(
-            src_ref=pack,
-            dst_ref=packs.at[d - 1],
-            send_sem=pack_send.at[d - 1],
-            recv_sem=pack_recv.at[d - 1],
-            device_id={"slab": lax.rem(l + d, n_slab)},
-            device_id_type=MESH,
-        )
-        copy.start()
-        pack_copies.append(copy)
-
     def use_packs():
         for copy in pack_copies:
             copy.wait()
@@ -407,7 +397,11 @@
         for d in range(n_slab):
             last = slice(pstride, pstride + 1)
             row = pack[last, 0:lp] if d == 0 else packs[d - 1, last, 0:lp]
-            coup[d] = jnp.where(own_col == row, chosen, 0.0)
+            used = jnp.where(own_col == row, chosen, 0.0)
+            high = used.astype(bf16)
+            coup[d, :, 0:lp] = high
+            coup[d, :, lp : 2 * lp] = high
+            coup[d, :, 2 * lp : 3 * lp] = (used - high.astype(f32)).astype(bf16)
         slot = lax.broadcasted_iota(jnp.int32, (flp, EDGE), 0).astype(f32) + 1.0
         for b in range(2):
             d = 1 if b == 0 else n_slab - 1
@@ -495,17 +489,19 @@
             marg_copies = send_margin(1)
             pl.loop(0, tiles // group)(take_cells(yb, False))
             local_part()
-        scatter()
+        scatter(step)
 
         if step == 0:
-            place_projectors(early, cells)
             use_packs()
         coupled = jnp.zeros((width, lp), f32)
         for d in range(n_slab):
             if d > 0:
                 marg_copies[d - 1].wait()
+            whole = marg[step, d]
+            high = whole.astype(bf16)
+            low = (whole - high.astype(f32)).astype(bf16)
             coupled += lax.dot_general(
-                marg[step, d], coup[d], NT, precision=lax.Precision.HIGHEST, preferred_element_type=f32
+                jnp.concatenate([high, low, high], axis=1), coup[d], NT, preferred_element_type=f32
             )
         coupled = coupled.astype(bf16)
         for b in range(blocks):
@@ -607,7 +603,7 @@
             pltpu.VMEM((up(cells, 8), op), f32),
             pltpu.VMEM((2 * fsp, 2 * flp), bf16),
             pltpu.VMEM((others, pstride + 16, wide), f32),
-            pltpu.VMEM((n_slab, lp, lp), f32),
+            pltpu.VMEM((n_slab, lp, 3 * lp), bf16),
             pltpu.VMEM((npad // BLK * width, BLK), bf16),
             pltpu.VMEM((cells * width, op), bf16),
             pltpu.VMEM((cells * width, op), f32),

time: 28.1 us -> 26.5 us (0.943)
  Pallas kernels: 27 us -> 25.4 us
    pallas_call x1, Pallas kernels: 27 us -> 25.4 us  [shards(): pl.pallas_call(functools.partial(kernel, dims), out_shape=pltpu.VMEM((wid...]
where the time goes in v4:
time: 26.5 us; the launch traced here: 26.3 us
  Pallas kernels  25.4 us (96%)
  local copies, waits for them, and re-layouts  0.85 us (3%)
    pallas_call x1, Pallas kernels, shards(): pl.pallas_call(functools.partial(kernel, dims), out_shape=pltpu.VMEM((wid...  25.4 us
    unnamed x1, local copies, waits for them, and re-layouts  0.85 us

profile of v4, /device:TPU:0, one launch (start us, length us, event | category | flops | bytes accessed | tf_op | source)
XLA Modules:
  0.0 26.3 jit_solution(3231409547216116161)
XLA Ops:
  0.0 25.4 %shard_map.100 = f32[64,2601]{1,0:T(8,128)S(1)} custom-call(bf16[64,2601]{1,0:T(8,128)(2,1)} %y_hbm.1, bf16[729,729]{1,0:T(8,128)(2,1)} %kin_hbm.1, f32[4]{0:T(128)} %scale_hbm.1, f32[4,729]{1,0:T(4,128)} %pot_hbm.1, s32[4,729]{1,0:T(4,128)} %cn_hbm.1, s32[2,289]{1,0:T(2,128)} %fs_hbm.1, s32[2,153]{1,0:T(2,128)} %fl_hbm.1, bf16[18,4,729]{2,1,0:T(4,128)(2,1)} %bitcast.2, ...), custom_call_target="tpu_custom_call" | custom-call | tf_op jit(solution)/shard_map/pallas_call | solution.py:581
  25.4 0.8 %copy.12 = f32[64,2601]{1,0:T(8,128)} copy(f32[64,2601]{1,0:T(8,128)S(1)} %shard_map.100) | data formatting | bytes 1331712

commit v5 on v4

--- a/solution.py
+++ b/solution.py
@@ -211,7 +211,7 @@
 
     per_cell = op // BLK
     tiles = cells * per_cell
-    group = max(g for g in (1, 2, 4) if tiles % g == 0)
+    group = max(g for g in (1, 2, 3, 6) if tiles % g == 0)
 
     def take_cells(source, build):
         def body(i):
@@ -347,9 +347,11 @@
             tot[rows, :] = total.astype(bf16)
 
     def scatter(step):
-        def one(c, fresh):
-            row = c * width if isinstance(c, int) else pl.multiple_of(c * width, width)
-            low = c * pstride if isinstance(c, int) else pl.multiple_of(c * pstride, pstride)
+        pair = 2 if cells % 2 == 0 else 1
+
+        def one(c):
+            row = pl.multiple_of(c * width, width)
+            low = pl.multiple_of(c * pstride, pstride)
             pieces = []
             for n in range(per_cell):
                 at = tile(c * op + n * BLK)
@@ -361,17 +363,17 @@
             each = width if step else width + pstride
             for b in range(blocks):
                 rows = slice(b * width, (b + 1) * width)
-                part = result[b * each : b * each + width]
-                asm[rows, :] = part if fresh else asm[rows, :] + part
+                asm[rows, :] += result[b * each : b * each + width]
                 if step == 0:
                     to = pl.ds(b * lp + low, pstride)
                     pn[to, :] = result[b * each + width : (b + 1) * each].astype(bf16)
 
-        one(0, True)
-
-        @pl.loop(1, cells)
+        asm[...] = jnp.zeros(asm.shape, f32)
+
+        @pl.loop(0, cells // pair)
         def _(c):
-            one(c, False)
+            for u in range(pair):
+                one(pair * c + u)
 
     margin_of(0)
     marg_copies = send_margin(0)

time: 26.5 us -> 25.6 us (0.966)
  Pallas kernels: 25.4 us -> 24.5 us
    pallas_call x1, Pallas kernels: 25.4 us -> 24.5 us  [shards(): pl.pallas_call(functools.partial(kernel, dims), out_shape=pltpu.VMEM((wid...]
where the time goes in v5:
time: 25.6 us; the launch traced here: 25.3 us
  Pallas kernels  24.5 us (96%)
  local copies, waits for them, and re-layouts  0.85 us (3%)
    pallas_call x1, Pallas kernels, shards(): pl.pallas_call(functools.partial(kernel, dims), out_shape=pltpu.VMEM((wid...  24.5 us
    unnamed x1, local copies, waits for them, and re-layouts  0.85 us

profile of v5, /device:TPU:0, one launch (start us, length us, event | category | flops | bytes accessed | tf_op | source)
XLA Modules:
  0.0 25.3 jit_solution(15895482327627237915)
XLA Ops:
  0.0 24.5 %shard_map.100 = f32[64,2601]{1,0:T(8,128)S(1)} custom-call(bf16[64,2601]{1,0:T(8,128)(2,1)} %y_hbm.1, bf16[729,729]{1,0:T(8,128)(2,1)} %kin_hbm.1, f32[4]{0:T(128)} %scale_hbm.1, f32[4,729]{1,0:T(4,128)} %pot_hbm.1, s32[4,729]{1,0:T(4,128)} %cn_hbm.1, s32[2,289]{1,0:T(2,128)} %fs_hbm.1, s32[2,153]{1,0:T(2,128)} %fl_hbm.1, bf16[18,4,729]{2,1,0:T(4,128)(2,1)} %bitcast.2, ...), custom_call_target="tpu_custom_call" | custom-call | tf_op jit(solution)/shard_map/pallas_call | solution.py:583
  24.5 0.8 %copy.12 = f32[64,2601]{1,0:T(8,128)} copy(f32[64,2601]{1,0:T(8,128)S(1)} %shard_map.100) | data formatting | bytes 1331712

commit v6 on v5

--- a/solution.py
+++ b/solution.py
@@ -61,6 +61,7 @@
     tot,
     asm,
     field,
+    origin,
     outg,
     in_slab,
     inc,
@@ -211,23 +212,27 @@
 
     per_cell = op // BLK
     tiles = cells * per_cell
-    group = max(g for g in (1, 2, 3, 6) if tiles % g == 0)
-
-    def take_cells(source, build):
+    group = max(g for g in range(1, 13) if tiles % g == 0)
+
+    def take_cells(source):
         def body(i):
             for u in range(group):
                 j = i * group + u
                 at = tile(j * BLK)
-                if build:
-                    hot[:, at] = low_part(at)
                 row = pl.ds(pl.multiple_of(j // per_cell * width, width), width)
                 vals[row, tile(j % per_cell * BLK)] = gather(source, at)
 
         return body
 
+    @pl.loop(0, cells)
+    def _(k):
+        for u in range(per_cell):
+            at = tile((per_cell * k + u) * BLK)
+            hot[:, at] = low_part(at)
+
     for k in range(fp // BLK):
-        at = tile(jp + k * BLK)
-        hot[:, at] = low_part(at)
+        hot[:, tile(jp + k * BLK)] = low_part(tile(jp + k * BLK))
+
     slab_row = idx[0:1, jp + o_sl : jp + o_sl + 2 * flp].astype(f32)
     slab_row = jnp.where(slab_row < 0, -2.0, slab_row)
     for k in range(2 * fsp // 128):
@@ -251,6 +256,8 @@
         pp[c * pstride : c * pstride + nproj, c * op : c * op + order] = pr_ref[:, c, :]
     for i in (1, 2, 3):
         loads[i].wait()
+    origin[...] = yb[...]
+    field[...] = yb[...].astype(f32)
     kin[...] = jnp.zeros(kin.shape, bf16)
     kin[0:order, 0:order] = kin_ref[...]
     pot[...] = jnp.zeros(pot.shape, f32)
@@ -286,7 +293,6 @@
         spots = jnp.where(spot_row == i, listed[0:8], spots)
     pack[pstride + 8 :, 0:EDGE] = spots
 
-    pl.loop(0, 1)(take_cells(yb, True))
     pl.semaphore_wait(barrier, greeted)
     pack_copies = []
     for d in range(1, n_slab):
@@ -301,11 +307,9 @@
         copy.start()
         pack_copies.append(copy)
 
-    pl.loop(1, tiles // group)(take_cells(yb, True))
-
-    def margin_of(step):
+    def margin_of(step, first):
         margin = jnp.zeros((width, lp), f32)
-        if step == 0:
+        if first:
             for c in range(cells):
                 margin += lax.dot_general(
                     vals[c * width : (c + 1) * width, :],
@@ -322,9 +326,8 @@
                     preferred_element_type=f32,
                 )
         marg[step, 0] = margin
-        return margin
-
-    def send_margin(step):
+
+    def margin_copies(step):
         copies = []
         for d in range(1, n_slab):
             copy = pltpu.make_async_remote_copy(
@@ -335,7 +338,6 @@
                 device_id={"slab": lax.rem(l + d, n_slab)},
                 device_id_type=MESH,
             )
-            copy.start()
             copies.append(copy)
         return copies
 
@@ -346,27 +348,16 @@
             total = scale_ref[c] * kinv[rows, :] + pot[c : c + 1, :] * vals[rows, :].astype(f32)
             tot[rows, :] = total.astype(bf16)
 
-    def scatter(step):
-        pair = 2 if cells % 2 == 0 else 1
+    def scatter():
+        pair = max(g for g in range(1, 5) if cells % g == 0)
 
         def one(c):
             row = pl.multiple_of(c * width, width)
-            low = pl.multiple_of(c * pstride, pstride)
             pieces = []
             for n in range(per_cell):
-                at = tile(c * op + n * BLK)
                 value = tot[pl.ds(row, width), tile(n * BLK)]
-                if step == 0:
-                    value = jnp.concatenate([value, pp[pl.ds(low, pstride), at]], axis=0)
-                pieces.append((value, at))
-            result = spread(pieces)
-            each = width if step else width + pstride
-            for b in range(blocks):
-                rows = slice(b * width, (b + 1) * width)
-                asm[rows, :] += result[b * each : b * each + width]
-                if step == 0:
-                    to = pl.ds(b * lp + low, pstride)
-                    pn[to, :] = result[b * each + width : (b + 1) * each].astype(bf16)
+                pieces.append((value, tile(c * op + n * BLK)))
+            asm[...] += spread(pieces)
 
         asm[...] = jnp.zeros(asm.shape, f32)
 
@@ -375,9 +366,21 @@
             for u in range(pair):
                 one(pair * c + u)
 
-    margin_of(0)
-    marg_copies = send_margin(0)
-    local_part()
+    def place_projectors():
+        turn = 2 if cells % 2 == 0 else 1
+
+        @pl.loop(0, cells // turn)
+        def _(h):
+            for u in range(turn):
+                c = h * turn + u
+                row = pl.ds(pl.multiple_of(c * pstride, pstride), pstride)
+                placed = spread(
+                    [(pp[row, tile(c * op + n * BLK)], tile(c * op + n * BLK)) for n in range(per_cell)]
+                ).astype(bf16)
+                for b in range(blocks):
+                    to = pl.ds(pl.multiple_of(b * lp + c * pstride, pstride), pstride)
+                    pn[to, :] = placed[b * pstride : (b + 1) * pstride]
+
     def use_packs():
         for copy in pack_copies:
             copy.wait()
@@ -485,16 +488,34 @@
         for k in range(first // BLK, last // BLK):
             outg[step, :, tile(k * BLK)] = gather(yb, tile(jp + k * BLK))
 
-    for step in range(2):
-        if step == 1:
-            margin_of(1)
-            marg_copies = send_margin(1)
-            pl.loop(0, tiles // group)(take_cells(yb, False))
-            local_part()
-        scatter(step)
-
-        if step == 0:
+    @pl.loop(0, 2)
+    def _(step):
+        marg_copies = margin_copies(step)
+        later = (step > 0).astype(f32)
+
+        @pl.when(step > 0)
+        def _():
+            margin_of(step, False)
+            for copy in marg_copies:
+                copy.start()
+
+        pl.loop(0, tiles // group)(take_cells(yb))
+
+        @pl.when(step == 0)
+        def _():
+            margin_of(step, True)
+            for copy in marg_copies:
+                copy.start()
+
+        local_part()
+
+        scatter()
+
+        @pl.when(step == 0)
+        def _():
+            place_projectors()
             use_packs()
+
         coupled = jnp.zeros((width, lp), f32)
         for d in range(n_slab):
             if d > 0:
@@ -515,36 +536,19 @@
             yb[rows, :] = whole.astype(bf16)
 
         moves = exchange(step)
-
-        if step == 0:
-            for b in range(blocks):
-                rows = slice(b * width, (b + 1) * width)
-                count = min(BLK, nodes - b * BLK)
-                field[rows, 0:count] = asm[rows, 0:count] - filter_centre * y_ref[
-                    :, b * BLK : b * BLK + count
-                ].astype(f32)
-                if count < BLK:
-                    field[rows, count:] = jnp.zeros((width, BLK - count), f32)
-            fresh = (field[...] + finish(step, moves)) / filter_half
-            field[...] = fresh
-            yb[...] = fresh.astype(bf16)
-        else:
-            for b in range(blocks):
-                rows = slice(b * width, (b + 1) * width)
-                count = min(BLK, nodes - b * BLK)
-                start = y_ref[:, b * BLK : b * BLK + count].astype(f32)
-                asm[rows, 0:count] = (
-                    2.0 / filter_half * asm[rows, 0:count]
-                    - 2.0 * filter_centre / filter_half * field[rows, 0:count]
-                    - start
-                )
-            added = finish(step, moves)
-            for b in range(blocks):
-                rows = slice(b * width, (b + 1) * width)
-                count = min(BLK, nodes - b * BLK)
-                out_ref[:, b * BLK : b * BLK + count] = (
-                    asm[rows, 0:count] + 2.0 / filter_half * added[rows, 0:count]
-                )
+        gain = (1.0 + later) / filter_half
+        asm[...] = (
+            gain * asm[...]
+            - gain * filter_centre * field[...]
+            - later * origin[...].astype(f32)
+        )
+        fresh = asm[...] + gain * finish(step, moves)
+        field[...] = fresh
+        yb[...] = fresh.astype(bf16)
+
+    for b in range(blocks):
+        count = min(BLK, nodes - b * BLK)
+        out_ref[:, b * BLK : b * BLK + count] = field[b * width : (b + 1) * width, 0:count]
 
 
 def shards(
@@ -612,6 +616,7 @@
             pltpu.VMEM((cells * width, op), bf16),
             pltpu.VMEM((npad // BLK * width, BLK), f32),
             pltpu.VMEM((npad // BLK * width, BLK), f32),
+            pltpu.VMEM((npad // BLK * width, BLK), bf16),
             pltpu.VMEM((2, width, fp), bf16),
             pltpu.VMEM((2, 2, width, flp), bf16),
             pltpu.VMEM((2, width, fp), bf16),

time: 25.6 us -> 25.3 us (0.988)
  Pallas kernels: 24.5 us -> 24.2 us
where the time goes in v6:
time: 25.3 us; the launch traced here: 25.1 us
  Pallas kernels  24.2 us (96%)
  local copies, waits for them, and re-layouts  0.85 us (3%)
    pallas_call x1, Pallas kernels, shards(): pl.pallas_call(functools.partial(kernel, dims), out_shape=pltpu.VMEM((wid...  24.2 us
    unnamed x1, local copies, waits for them, and re-layouts  0.85 us

profile of v6, /device:TPU:0, one launch (start us, length us, event | category | flops | bytes accessed | tf_op | source)
XLA Modules:
  0.0 25.1 jit_solution(7512245424083014869)
XLA Ops:
  0.0 24.2 %shard_map.100 = f32[64,2601]{1,0:T(8,128)S(1)} custom-call(bf16[64,2601]{1,0:T(8,128)(2,1)} %y_hbm.1, bf16[729,729]{1,0:T(8,128)(2,1)} %kin_hbm.1, f32[4]{0:T(128)} %scale_hbm.1, f32[4,729]{1,0:T(4,128)} %pot_hbm.1, s32[4,729]{1,0:T(4,128)} %cn_hbm.1, s32[2,289]{1,0:T(2,128)} %fs_hbm.1, s32[2,153]{1,0:T(2,128)} %fl_hbm.1, bf16[18,4,729]{2,1,0:T(4,128)(2,1)} %bitcast.2, ...), custom_call_target="tpu_custom_call" | custom-call | tf_op jit(solution)/shard_map/pallas_call | solution.py:587
  24.3 0.8 %copy.12 = f32[64,2601]{1,0:T(8,128)} copy(f32[64,2601]{1,0:T(8,128)S(1)} %shard_map.100) | data formatting | bytes 1331712

commit v7 on v6

--- a/solution.py
+++ b/solution.py
@@ -349,22 +349,13 @@
             tot[rows, :] = total.astype(bf16)
 
     def scatter():
-        pair = max(g for g in range(1, 5) if cells % g == 0)
-
-        def one(c):
-            row = pl.multiple_of(c * width, width)
-            pieces = []
-            for n in range(per_cell):
-                value = tot[pl.ds(row, width), tile(n * BLK)]
-                pieces.append((value, tile(c * op + n * BLK)))
-            asm[...] += spread(pieces)
-
-        asm[...] = jnp.zeros(asm.shape, f32)
-
-        @pl.loop(0, cells // pair)
-        def _(c):
-            for u in range(pair):
-                one(pair * c + u)
+        asm[...] = spread(
+            [
+                (tot[c * width : (c + 1) * width, tile(n * BLK)], tile(c * op + n * BLK))
+                for c in range(cells)
+                for n in range(per_cell)
+            ]
+        )
 
     def place_projectors():
         turn = 2 if cells % 2 == 0 else 1

time: 25.3 us -> 25.3 us (level)
  no operation moved by 1% of the time
where the time goes in v7:
time: 25.3 us; the launch traced here: 25.1 us
  Pallas kernels  24.2 us (96%)
  local copies, waits for them, and re-layouts  0.85 us (3%)
    pallas_call x1, Pallas kernels, shards(): pl.pallas_call(functools.partial(kernel, dims), out_shape=pltpu.VMEM((wid...  24.2 us
    unnamed x1, local copies, waits for them, and re-layouts  0.85 us

profile of v7, /device:TPU:0, one launch (start us, length us, event | category | flops | bytes accessed | tf_op | source)
XLA Modules:
  0.0 25.1 jit_solution(12894833474912083642)
XLA Ops:
  0.0 24.2 %shard_map.100 = f32[64,2601]{1,0:T(8,128)S(1)} custom-call(bf16[64,2601]{1,0:T(8,128)(2,1)} %y_hbm.1, bf16[729,729]{1,0:T(8,128)(2,1)} %kin_hbm.1, f32[4]{0:T(128)} %scale_hbm.1, f32[4,729]{1,0:T(4,128)} %pot_hbm.1, s32[4,729]{1,0:T(4,128)} %cn_hbm.1, s32[2,289]{1,0:T(2,128)} %fs_hbm.1, s32[2,153]{1,0:T(2,128)} %fl_hbm.1, bf16[18,4,729]{2,1,0:T(4,128)(2,1)} %bitcast.2, ...), custom_call_target="tpu_custom_call" | custom-call | tf_op jit(solution)/shard_map/pallas_call | solution.py:578
  24.3 0.8 %copy.12 = f32[64,2601]{1,0:T(8,128)} copy(f32[64,2601]{1,0:T(8,128)S(1)} %shard_map.100) | data formatting | bytes 1331712

commit v8 on v6

--- a/solution.py
+++ b/solution.py
@@ -476,13 +476,12 @@
     def finish(step, moves):
         for sends, gets, copy in moves:
             pl.when(gets)(copy.wait_recv)
-        for sends, gets, copy in moves:
-            pl.when(sends)(copy.wait_send)
         for b in range(2):
             part = slice(o_sl + b * flp, o_sl + (b + 1) * flp)
             corner = lax.dot_general(in_edge[step, b], spot[b], NT, preferred_element_type=f32)
             inc[step, :, part] = (in_slab[step, b].astype(f32) + corner).astype(bf16)
-        return spread([(inc[step, :, tile(k * BLK)], tile(jp + k * BLK)) for k in range(fp // BLK)])
+        halo = spread([(inc[step, :, tile(k * BLK)], tile(jp + k * BLK)) for k in range(fp // BLK)])
+        return halo
 
     def take_faces(step, first, last):
         for k in range(first // BLK, last // BLK):
@@ -545,6 +544,8 @@
         fresh = asm[...] + gain * finish(step, moves)
         field[...] = fresh
         yb[...] = fresh.astype(bf16)
+        for sends, gets, copy in moves:
+            pl.when(sends)(copy.wait_send)
 
     for b in range(blocks):
         count = min(BLK, nodes - b * BLK)

time: 25.3 us -> 25.4 us (level)
  no operation moved by 1% of the time
where the time goes in v8:
time: 25.4 us; the launch traced here: 25.1 us
  Pallas kernels  24.3 us (96%)
  local copies, waits for them, and re-layouts  0.85 us (3%)
    pallas_call x1, Pallas kernels, shards(): pl.pallas_call(functools.partial(kernel, dims), out_shape=pltpu.VMEM((wid...  24.3 us
    unnamed x1, local copies, waits for them, and re-layouts  0.85 us

profile of v8, /device:TPU:0, one launch (start us, length us, event | category | flops | bytes accessed | tf_op | source)
XLA Modules:
  0.0 25.1 jit_solution(11468083649769988291)
XLA Ops:
  0.0 24.3 %shard_map.100 = f32[64,2601]{1,0:T(8,128)S(1)} custom-call(bf16[64,2601]{1,0:T(8,128)(2,1)} %y_hbm.1, bf16[729,729]{1,0:T(8,128)(2,1)} %kin_hbm.1, f32[4]{0:T(128)} %scale_hbm.1, f32[4,729]{1,0:T(4,128)} %pot_hbm.1, s32[4,729]{1,0:T(4,128)} %cn_hbm.1, s32[2,289]{1,0:T(2,128)} %fs_hbm.1, s32[2,153]{1,0:T(2,128)} %fl_hbm.1, bf16[18,4,729]{2,1,0:T(4,128)(2,1)} %bitcast.2, ...), custom_call_target="tpu_custom_call" | custom-call | tf_op jit(solution)/shard_map/pallas_call | solution.py:588
  24.3 0.8 %copy.12 = f32[64,2601]{1,0:T(8,128)} copy(f32[64,2601]{1,0:T(8,128)S(1)} %shard_map.100) | data formatting | bytes 1331712
